TPU v7x, 1024 devices: a whole 8x8x8 slice. The times are simulated.
1024 devices in a mesh: vol: 16 (over x, core), surf: 64 (over z, y).
Axes of the slice: x: 8, y: 8, z: 8, core: 2. Of those that a mesh axis runs over, the one named last changes fastest.
Arguments:
- points: float32 [3, 131072], P(None, ('vol', 'surf')), may hold values from -1 to 1
- surface_points: float32 [3, 65536], P(None, 'surf'), may hold values from -1 to 1
- displacement: float32 [3, 65536], P(None, 'surf'), may hold values from -6 to 6
- rotation: float32 [3, 65536], P(None, 'surf'), may hold values from -3 to 3
- halo_index: int32 [32768], P(('vol', 'surf')), may hold values from 0 to 127
- connectivity: int32 [4, 524288], P(None, ('vol', 'surf')), may hold values from 0 to 191
Outputs:
- node_motion: float32 [3, 131072], P(None, ('vol', 'surf'))
- swept: float32 [524288], P(('vol', 'surf'))
All inputs are finite; a program needn't handle non-finite values.
Results may differ from a plain program's by a relative error of at most 0.0003.
Values sent between devices are 32-bit elements; how exact they have to be, the bound alone decides.
No kernel may reach another device: no remote copies, remote signals or barrier semaphores. Data moves between devices by JAX's collectives and lax.ppermute only.
A program may use at most 32 MiB of HBM per device.

v0:
```python
import math

import jax
import jax.numpy as jnp
from jax import lax
from jax.sharding import PartitionSpec as P

SOFTENING = 0.01


def with_halo(shard, sides, width):
    for axis, dim in sides:
        size, length = (lax.axis_size(axis), shard.shape[dim])
        up = [(i, (i + 1) % size) for i in range(size)]
        down = [(j, i) for i, j in up]
        last = lax.slice_in_dim(shard, length - width, length, axis=dim)
        initial = lax.slice_in_dim(shard, 0, width, axis=dim)
        before = lax.ppermute(last, axis, up)
        after = lax.ppermute(initial, axis, down)
        shard = jnp.concatenate([before, shard, after], axis=dim)
    return shard


def surface_terms(surface_points, displacement, rotation):
    rotated = jnp.cross(rotation, surface_points, axis=0)
    unit_row = jnp.ones_like(surface_points[0:1])
    return jnp.concatenate([displacement - rotated, rotation, unit_row], axis=0)


def pair_weight(node_points, anchors):
    gap_x = node_points[0][:, None] - anchors[0][None, :]
    gap_y = node_points[1][:, None] - anchors[1][None, :]
    gap_z = node_points[2][:, None] - anchors[2][None, :]
    spread = gap_x * gap_x + gap_y * gap_y + gap_z * gap_z + SOFTENING
    return lax.rsqrt(spread) / spread


def weighted_sums(node_points, anchors, term_rows):
    weight = pair_weight(node_points, anchors)
    return jnp.einsum("ns,cs->cn", weight, term_rows, precision=lax.Precision.HIGHEST)


def node_shift(node_points, totals):
    return (totals[0:3] + jnp.cross(totals[3:6], node_points, axis=0)) / totals[6:7]


def swept_volume(corners):
    initial = corners[0:3]
    motion = corners[3:6]
    halfway = initial + 0.5 * motion
    face_list = ((1, 2, 3), (0, 3, 2), (0, 1, 3), (0, 2, 1))
    swept_sum = jnp.zeros(corners.shape[2:], corners.dtype)
    for first, second, third in face_list:
        normal = 0.5 * jnp.cross(
            halfway[:, second] - halfway[:, first], halfway[:, third] - halfway[:, first], axis=0
        )
        average = (motion[:, first] + motion[:, second] + motion[:, third]) / 3.0
        swept_sum = swept_sum + jnp.sum(average * normal, axis=0)
    return swept_sum


def shards(points, surface_points, displacement, rotation, halo_index, connectivity):
    term_rows = surface_terms(surface_points, displacement, rotation)
    node_count = points.shape[1]
    gathered = lax.all_gather(points, "surf", axis=1, tiled=True)
    tile_width = gathered.shape[1]
    block_size = math.gcd(tile_width, 2048)
    block_count = tile_width // block_size
    blocks = gathered.reshape(3, block_count, block_size).transpose(1, 0, 2)
    partial_value = lax.map(
        lambda block_points: weighted_sums(block_points, surface_points, term_rows), blocks
    )
    partial_value = partial_value.transpose(1, 0, 2).reshape(7, tile_width)
    reduced = lax.psum(partial_value, "surf")
    totals = lax.dynamic_slice_in_dim(reduced, lax.axis_index("surf") * node_count, node_count, 1)
    node_motion = node_shift(points, totals)
    node_state = jnp.concatenate([points, node_motion], axis=0)
    rim_nodes = node_state[:, halo_index]
    rim_width = halo_index.shape[0]
    bordered = with_halo(rim_nodes, ((("vol", "surf"), 1),), rim_width)
    extended = jnp.concatenate(
        [bordered[:, :rim_width], node_state, bordered[:, 2 * rim_width :]], axis=1
    )
    corners = extended[:, connectivity]
    return (node_motion, swept_volume(corners))


def solution(mesh):
    in_specs = (
        P(None, ("vol", "surf")),
        P(None, "surf"),
        P(None, "surf"),
        P(None, "surf"),
        P(("vol", "surf")),
        P(None, ("vol", "surf")),
    )
    out_specs = (P(None, ("vol", "surf")), P(("vol", "surf")))
    return jax.shard_map(shards, mesh=mesh, in_specs=in_specs, out_specs=out_specs, check_vma=False)
```

profile of v0, /device:TPU:14, one launch (start us, length us, event | category | flops | bytes accessed | tf_op | source)
XLA Modules:
  0.0 309.3 jit_solution(13494874208358355206)
XLA Ops:
  7.2 63.3 %all_gather.3 = f32[3,8192]{1,0:T(4,128)S(1)} all-gather(f32[3,128]{1,0:T(4,128)} %param.10), channel_id=1, replica_groups=mesh['vol'=16,'surf'=64] {'surf'}, dimensions={1}, use_global_device_ids=true | all-gather | bytes 99840 | tf_op jit(solution)/shard_map/all_gather | solution.py:65
  70.5 0.1 pad.22.clone
  70.6 0.9 subtract_bitcast_fusion.7
  71.5 0.7 maximum_subtract_fusion
  72.3 0.8 maximum_maximum_fusion
  73.1 48.5 %while.10 = (s32[]{:T(128)}, f32[4,7,2048]{2,1,0:T(8,128)}, f32[4,3,2048]{2,1,0:T(4,128)S(1)}, f32[3,1024]{1,0:T(4,128)}, f32[7,1024]{1,0:T(8,128)S(1)}, /*index=5*/s32[]{:T(128)}, s32[]{:T(128)}, s32[]{}, s32[]{}) while((s32[]{:T(128)}, f32[4,7,2048]{2,1,0:T(8,128)}, f32[4,3,2048]{2,1,0:T(4,128)S(1)}, f32[3,1024]{1,0:T(4,128)}, ...), condition=%wide.region_1.2_spmd, body=%wide.region_0.1_spmd.sunk | while | flops 197132288 | bytes 204941 | solution.py:70
  73.1 0.8 fusion.28
  74.0 11.2 %fusion.29 = f32[4,7,2048]{2,1,0:T(8,128)} fusion(f32[4,7,2048]{2,1,0:T(8,128)} %get-tuple-element.131, s32[]{:T(128)S(6)} %copy.34, f32[7,1024]{1,0:T(8,128)S(1)} %get-tuple-element.143, f32[1024]{0:T(1024)S(1)} %bitcast.153, f32[2048]{0:T(1024)S(1)} %bitcast.151, f32[1024]{0:T(1024)S(1)} %bitcast.154, f32[2048]{0:T(1024)S(1)} %bitcast.150, ...), kind=kOutput, calls=%fused_computation.12.clone.1 | convolution fusion | flops 197132288 | bytes 131076 | tf_op jit(solution)/shard_map/while/body/eval_jaxpr/ns,cs->cn/dot_general | solution.py:40
  85.2 0.8 fusion.28
  86.1 11.2 %fusion.29 = f32[4,7,2048]{2,1,0:T(8,128)} fusion(f32[4,7,2048]{2,1,0:T(8,128)} %get-tuple-element.131, s32[]{:T(128)S(6)} %copy.34, f32[7,1024]{1,0:T(8,128)S(1)} %get-tuple-element.143, f32[1024]{0:T(1024)S(1)} %bitcast.153, f32[2048]{0:T(1024)S(1)} %bitcast.151, f32[1024]{0:T(1024)S(1)} %bitcast.154, f32[2048]{0:T(1024)S(1)} %bitcast.150, ...), kind=kOutput, calls=%fused_computation.12.clone.1 | convolution fusion | flops 197132288 | bytes 131076 | tf_op jit(solution)/shard_map/while/body/eval_jaxpr/ns,cs->cn/dot_general | solution.py:40
  97.3 0.8 fusion.28
  98.2 11.2 %fusion.29 = f32[4,7,2048]{2,1,0:T(8,128)} fusion(f32[4,7,2048]{2,1,0:T(8,128)} %get-tuple-element.131, s32[]{:T(128)S(6)} %copy.34, f32[7,1024]{1,0:T(8,128)S(1)} %get-tuple-element.143, f32[1024]{0:T(1024)S(1)} %bitcast.153, f32[2048]{0:T(1024)S(1)} %bitcast.151, f32[1024]{0:T(1024)S(1)} %bitcast.154, f32[2048]{0:T(1024)S(1)} %bitcast.150, ...), kind=kOutput, calls=%fused_computation.12.clone.1 | convolution fusion | flops 197132288 | bytes 131076 | tf_op jit(solution)/shard_map/while/body/eval_jaxpr/ns,cs->cn/dot_general | solution.py:40
  109.5 0.8 fusion.28
  110.3 11.2 %fusion.29 = f32[4,7,2048]{2,1,0:T(8,128)} fusion(f32[4,7,2048]{2,1,0:T(8,128)} %get-tuple-element.131, s32[]{:T(128)S(6)} %copy.34, f32[7,1024]{1,0:T(8,128)S(1)} %get-tuple-element.143, f32[1024]{0:T(1024)S(1)} %bitcast.153, f32[2048]{0:T(1024)S(1)} %bitcast.151, f32[1024]{0:T(1024)S(1)} %bitcast.154, f32[2048]{0:T(1024)S(1)} %bitcast.150, ...), kind=kOutput, calls=%fused_computation.12.clone.1 | convolution fusion | flops 197132288 | bytes 131076 | tf_op jit(solution)/shard_map/while/body/eval_jaxpr/ns,cs->cn/dot_general | solution.py:40
  121.7 161.4 %all-reduce.2.cloned.1.call-done = f32[7,8192]{1,0:T(8,128)} async-done(((f32[7,8192]{1,0:T(8,128)}), f32[7,8192]{1,0:T(8,128)}) %all-reduce.2.cloned.1.call-update) | async-done | bytes 229392 | tf_op jit(solution)/shard_map/psum | solution.py:74
  283.1 0.7 constant_dynamic-slice_fusion.3
  283.9 0.1 copy.27
  284.0 0.6 gather_fusion
  284.6 2.6 collective-permute-start
  287.2 7.1 %collective-permute-start.1 = (f32[6,32]{0,1:T(8,128)S(1)}, f32[6,32]{0,1:T(8,128)S(1)}, u32[]{:S(2)}, u32[]{:S(2)}) collective-permute-start(f32[6,32]{0,1:T(8,128)S(1)} %bitcast.159), channel_id=1, source_target_pairs={{1,0},{2,1},{3,2},{4,3},{5,4},{6,5},{7,6},{8,7},{9,8},{10,9},{11,1... | collective-permute-start | bytes 2312 | tf_op jit(solution)/shard_map/ppermute | solution.py:19
  294.4 1.4 collective-permute-done.1
  295.8 5.5 %gather_fusion.1 = f32[2048,6]{1,0:T(8,128)S(1)} fusion(f32[6,192]{0,1:T(8,128)S(1)} %pad_maximum_fusion, s32[2048]{0:T(1024)S(1)} %broadcast_clamp_fusion), kind=kCustom, calls=%fused_computation.1 | custom fusion | bytes 106496 | tf_op jit(solution)/shard_map/gather | solution.py:84
  301.3 0.3 copy.29
  301.8 0.6 add_add_fusion
  (34 shorter events, 0.4 us)
Async XLA Ops:
  7.2 276.0 %all-reduce.2.cloned.1.call-start = ((), (), s32[]{:S(2)}) async-start(), calls=%async_computation | async-start | bytes 524288 | tf_op jit(solution)/shard_map/psum | solution.py:74
  73.1 48.6 %copy-start.1 = (s32[4,512]{1,0:T(4,128)S(1)}, s32[4,512]{1,0:T(4,128)}, u32[]{:S(2)}) copy-start(s32[4,512]{1,0:T(4,128)} %param.15) | copy-start | bytes 24580
  73.1 48.6 %copy-start.3 = (s32[32]{0:T(128)S(1)}, s32[32]{0:T(128)}, u32[]{:S(2)}) copy-start(s32[32]{0:T(128)} %param.14) | copy-start | bytes 388
  73.1 210.8 %copy-start = (f32[3,128]{1,0:T(4,128)S(1)}, f32[3,128]{1,0:T(4,128)}, u32[]{:S(2)}) copy-start(f32[3,128]{1,0:T(4,128)} %param.10) | copy-start | bytes 4612
  283.9 17.8 %copy-start.2 = (f32[3,128]{1,0:T(4,128)}, f32[3,128]{1,0:T(4,128)S(1)}, u32[]{:S(2)}) copy-start(f32[3,128]{1,0:T(4,128)S(1)} %fusion.21) | copy-start | bytes 4612
  284.6 9.8 %collective-permute-start = (f32[6,32]{0,1:T(8,128)S(1)}, f32[6,32]{0,1:T(8,128)S(1)}, u32[]{:S(2)}, u32[]{:S(2)}) collective-permute-start(f32[6,32]{0,1:T(8,128)S(1)} %bitcast.158), channel_id=1, source_target_pairs={{0,1},{1,2},{2,3},{3,4},{4,5},{5,6},{6,7},{7,8},{8,9},{9,10},{10,1... | collective-permute-start | bytes 2312 | tf_op jit(solution)/shard_map/ppermute | solution.py:18
  287.2 8.6 %collective-permute-start.1 = (f32[6,32]{0,1:T(8,128)S(1)}, f32[6,32]{0,1:T(8,128)S(1)}, u32[]{:S(2)}, u32[]{:S(2)}) collective-permute-start(f32[6,32]{0,1:T(8,128)S(1)} %bitcast.159), channel_id=1, source_target_pairs={{1,0},{2,1},{3,2},{4,3},{5,4},{6,5},{7,6},{8,7},{9,8},{10,9},{11,1... | collective-permute-start | bytes 2312 | tf_op jit(solution)/shard_map/ppermute | solution.py:19
Sparse Core Ops, SparseCore 0:
  121.7 161.3 all-reduce.1
where the time goes:
time: 312 us; the launch traced here: 309 us
  waiting for transfers between devices  163 us (52%)
  blocking collectives  63.3 us (20%)
  matrix products  45 us (14%)
  between operations  14.2 us (5%)
  local copies, waits for them, and re-layouts  10.8 us (3%)
  starting transfers between devices  9.82 us (3%)
  other arithmetic  3.23 us (1%)
    psum x1, waiting for transfers between devices, shards(): reduced = lax.psum(partial_value, 'surf')  161 us
    all_gather x1, blocking collectives, shards(): gathered = lax.all_gather(points, 'surf', axis=1, tiled=True)  63.3 us
    dot_general x4, matrix products, weighted_sums(): jnp.einsum('ns,cs->cn', weight, term_rows, precision=lax.Precision.HIGHEST)  45 us
    ppermute x1, starting transfers between devices, with_halo(): after = lax.ppermute(initial, axis, down)  7.14 us
  transfers between devices with their start and end apart: 3, of which 2 were waited for; matrix products, arithmetic and copies ran while one was open for 0% of the time, Pallas kernels for 0%

commit v1 on v0

v1 whole, which is shorter than its diff:
```python
import jax
import jax.numpy as jnp
from jax import lax
from jax.experimental import pallas as pl
from jax.experimental.pallas import tpu as pltpu
from jax.sharding import Mesh
from jax.sharding import PartitionSpec as P

SOFTENING = 0.01
F32 = jnp.float32
BF16 = jnp.bfloat16
SIDE = 8
LANES = 128
NODE_STEP = 384
SURF_STEP = 1024
NT = (((1,), (1,)), ((), ()))


def rows_of(shape):
    return lax.broadcasted_iota(jnp.int32, shape, 0)


def lanes_of(shape):
    return lax.broadcasted_iota(jnp.int32, shape, 1)


def cross3(a, b):
    return (
        a[1] * b[2] - a[2] * b[1],
        a[2] * b[0] - a[0] * b[2],
        a[0] * b[1] - a[1] * b[0],
    )


def in_three(value):
    high = value.astype(BF16).astype(F32)
    rest = value - high
    middle = rest.astype(BF16).astype(F32)
    return high, middle, rest - middle


def pick_lanes(table, index):
    spread = jnp.broadcast_to(index, table.shape)
    return jnp.take_along_axis(table, spread, axis=1, mode="promise_in_bounds")


def prepare_kernel(points, surface, displacement, rotation, halo, message, lent):
    at = [surface[i : i + 1, :] for i in range(3)]
    turn = [rotation[i : i + 1, :] for i in range(3)]
    rotated = cross3(turn, at)
    term = [displacement[i : i + 1, :] - rotated[i] for i in range(3)]
    body = jnp.concatenate(term + turn[:2] + at, axis=0)
    last = jnp.concatenate([turn[2][:, i * LANES : (i + 1) * LANES] for i in range(SIDE)], axis=0)
    whole = jnp.concatenate([body, last], axis=1)
    for i in range(SIDE):
        message[i] = whole
    table = jnp.concatenate([points[...], jnp.zeros((5, LANES), F32)], axis=0)
    lent[...] = pick_lanes(table, halo[0:1, :])


def sums_kernel(place, nodes, surface, message, near, left, right, terms, total, sums, spots):
    row = rows_of((SIDE, LANES))
    lane = lanes_of((SIDE, LANES))
    outer = jnp.where(
        lane < 32,
        nodes[0],
        pltpu.roll(nodes[SIDE - 1], 32, axis=1),
    )
    outer = pltpu.roll(outer, 5, axis=0)
    for block in range(SIDE + 1):
        value = nodes[block] if block < SIDE else outer
        square = value[5:6] * value[5:6] + value[6:7] * value[6:7] + value[7:8] * value[7:8] + SOFTENING
        side = jnp.where(row >= 5, -2.0 * value, jnp.where(row == 3, 1.0, jnp.where(row == 4, square, 0.0)))
        high, middle, low = in_three(side)
        stack = [high, high, high, middle, middle, low, middle, low]
        stack = jnp.concatenate(stack + [jnp.zeros_like(high)] * 8, axis=0)
        left[block * LANES : (block + 1) * LANES, :] = stack.T.astype(BF16)[:, :64]
    width = surface.shape[2] - LANES
    line = rows_of((SIDE, width))
    for part in range(SIDE):
        value = surface[part][:, :width]
        tail = surface[part][:, width:]
        tail = jnp.concatenate([tail[i : i + 1] for i in range(SIDE)], axis=1)
        square = value[5:6] * value[5:6] + value[6:7] * value[6:7] + value[7:8] * value[7:8]
        side = jnp.where(line >= 5, value, jnp.where(line == 3, square, jnp.where(line == 4, 1.0, 0.0)))
        high, middle, low = in_three(side)
        stack = jnp.concatenate([high, middle, low, high, middle, high, low, middle], axis=0)
        right[:, part * width : (part + 1) * width] = stack.astype(BF16)
        term = jnp.where(line < 5, value, jnp.where(line == 5, tail, jnp.where(line == 6, 1.0, 0.0)))
        high, middle, _ = in_three(term)
        terms[:, part * width : (part + 1) * width] = jnp.concatenate([high, middle], axis=0).astype(BF16)
    total[...] = jnp.zeros_like(total)
    across = right.shape[1] // SURF_STEP

    def step(i, carry):
        n = pl.multiple_of((i // across) * NODE_STEP, LANES)
        s = pl.multiple_of((i % across) * SURF_STEP, LANES)
        spread = jnp.dot(left[pl.ds(n, NODE_STEP), :], right[:, pl.ds(s, SURF_STEP)], preferred_element_type=F32)
        inverse = lax.rsqrt(spread)
        weight = inverse * inverse * inverse
        high = weight.astype(BF16)
        low = (weight - high.astype(F32)).astype(BF16)
        term = terms[:, pl.ds(s, SURF_STEP)]
        total[pl.ds(n, NODE_STEP), :] += lax.dot_general(
            high, term, NT, preferred_element_type=F32
        ) + lax.dot_general(low, term, NT, preferred_element_type=F32)
        return carry

    lax.fori_loop(0, (SIDE + 1) * LANES // NODE_STEP * across, step, 0)

    for block in range(SIDE + 1):
        both = total[block * LANES : (block + 1) * LANES, :]
        both = jnp.concatenate([both, jnp.zeros((LANES, LANES - 16), F32)], axis=1).T
        value = both[:SIDE] + both[SIDE : 2 * SIDE]
        if block < SIDE:
            message[block, :, :LANES] = value
            index = nodes[block][3:4].astype(jnp.int32)
            sums[block + 1] = pick_lanes(value, index)
            spots[block + 1] = pick_lanes(nodes[block], index)
        else:
            sums[0] = value
            sums[SIDE + 1] = pltpu.roll(value, LANES - 32, axis=1)
            spots[0] = outer
            spots[SIDE + 1] = pltpu.roll(outer, LANES - 32, axis=1)
    for block in range(SIDE):
        message[block, :, LANES:] = jnp.where(lane < 32, sums[block], pltpu.roll(sums[block + 2], 32, axis=1))
    here = place[0]
    near[:, :LANES] = nodes[here]
    near[:, LANES:] = jnp.where(lane < 32, spots[here], pltpu.roll(spots[here + 2], 32, axis=1))


def swept_kernel(received, near, cells, motion_out, swept_out):
    total = received[0]
    for i in range(1, SIDE):
        total = total + received[i]
    top = [total[i : i + 1] for i in range(3)]
    turn = [total[i : i + 1] for i in range(3, 6)]
    spot = [near[i : i + 1, :] for i in range(5, 8)]
    turned = cross3(turn, spot)
    motion = [(top[i] + turned[i]) / total[6:7] for i in range(3)]
    motion_out[...] = jnp.concatenate([m[:, :LANES] for m in motion], axis=0)
    table = jnp.concatenate(spot + motion + [jnp.zeros_like(spot[0])] * 2, axis=0)
    own, lent = table[:, :LANES], table[:, LANES:]
    count = cells.shape[1]
    for group in range(count // LANES):
        corner = []
        for a in range(4):
            index = cells[a : a + 1, group * LANES : (group + 1) * LANES]
            inside = (index >= 32) & (index < 160)
            from_own = pick_lanes(own, jnp.where(inside, index - 32, 0))
            from_lent = pick_lanes(lent, jnp.where(inside, 0, jnp.where(index < 32, index, index - 128)))
            corner.append(jnp.where(jnp.broadcast_to(inside, own.shape), from_own, from_lent))
        move = [[c[3 + i : 4 + i] for i in range(3)] for c in corner]
        half = [[c[i : i + 1] + 0.5 * c[3 + i : 4 + i] for i in range(3)] for c in corner]
        result = jnp.zeros((1, LANES), F32)
        for p, q, r in ((1, 2, 3), (0, 3, 2), (0, 1, 3), (0, 2, 1)):
            one = [half[q][i] - half[p][i] for i in range(3)]
            two = [half[r][i] - half[p][i] for i in range(3)]
            normal = cross3(one, two)
            for i in range(3):
                average = (move[p][i] + move[q][i] + move[r][i]) / 3.0
                result = result + average * (0.5 * normal[i])
        swept_out[group : group + 1, :] = result


def shards(points, surface, displacement, rotation, halo_index, connectivity):
    width = surface.shape[1]
    nodes = points.shape[1]
    lend = halo_index.shape[0]
    halo = jnp.pad(halo_index[None, :], ((0, 7), (0, nodes - lend)))
    message, lent = pl.pallas_call(
        prepare_kernel,
        out_shape=(
            jax.ShapeDtypeStruct((SIDE, 8, width + LANES), F32),
            jax.ShapeDtypeStruct((8, LANES), F32),
        ),
    )(points, surface, displacement, rotation, halo)
    blocks = lax.axis_size("vol") * SIDE * SIDE
    ends = []
    for b in range(SIDE - 1, blocks, SIDE):
        ends += [(b, (b + 1) % blocks), ((b + 1) % blocks, b)]
    outer = lax.ppermute(lent[:3], ("vol", "z", "y"), ends)
    surfaces = lax.all_to_all(message, "z", 0, 0)
    own = jnp.concatenate(
        [outer, halo[:1].astype(F32), jnp.zeros((1, nodes), F32), points], axis=0
    )
    around = lax.all_to_all(jnp.broadcast_to(own[None], (SIDE, 8, nodes)), "y", 0, 0)
    place = lax.axis_index("y").astype(jnp.int32).reshape(1)
    vmem = pl.BlockSpec(memory_space=pltpu.VMEM)
    partial, near = pl.pallas_call(
        sums_kernel,
        out_shape=(
            jax.ShapeDtypeStruct((SIDE, 8, 2 * LANES), F32),
            jax.ShapeDtypeStruct((8, 2 * LANES), F32),
        ),
        in_specs=[pl.BlockSpec(memory_space=pltpu.SMEM), vmem, vmem],
        out_specs=(vmem, vmem),
        scratch_shapes=[
            pltpu.VMEM(((SIDE + 1) * LANES, 64), BF16),
            pltpu.VMEM((64, SIDE * width), BF16),
            pltpu.VMEM((16, SIDE * width), BF16),
            pltpu.VMEM(((SIDE + 1) * LANES, 16), F32),
            pltpu.VMEM((SIDE + 2, 8, LANES), F32),
            pltpu.VMEM((SIDE + 2, 8, LANES), F32),
        ],
        compiler_params=pltpu.CompilerParams(vmem_limit_bytes=40 << 20),
    )(place, around, surfaces)
    received = lax.all_to_all(partial, "y", 0, 0)
    count = connectivity.shape[1]
    motion, swept = pl.pallas_call(
        swept_kernel,
        out_shape=(
            jax.ShapeDtypeStruct((3, nodes), F32),
            jax.ShapeDtypeStruct((count // LANES, LANES), F32),
        ),
    )(received, near, connectivity)
    return motion, swept.reshape(count)


def solution(mesh):
    split = Mesh(mesh.devices.reshape(mesh.devices.shape[0], SIDE, SIDE), ("vol", "z", "y"))
    nodes = ("vol", "z", "y")
    surface = P(None, ("z", "y"))
    in_specs = (P(None, nodes), surface, surface, surface, P(nodes), P(None, nodes))
    out_specs = (P(None, nodes), P(nodes))
    return jax.shard_map(shards, mesh=split, in_specs=in_specs, out_specs=out_specs, check_vma=False)
```

time: 312 us -> 89.6 us (0.29)
  waiting for transfers between devices: 163 us -> 14.4 us
  matrix products: 45 us -> 0 us
  blocking collectives: 63.3 us -> 21.8 us
  Pallas kernels: 0 us -> 23.6 us
  starting transfers between devices: 9.82 us -> 26.6 us
  between operations: 14.2 us -> 0.68 us
  local copies, waits for them, and re-layouts: 10.8 us -> 2.01 us
  other arithmetic: 3.23 us -> 0.08 us
    psum x1 -> x0, waiting for transfers between devices: 161 us -> none  [shards(): reduced = lax.psum(partial_value, 'surf')]
    all_gather x1 -> x0, blocking collectives: 63.3 us -> none  [shards(): gathered = lax.all_gather(points, 'surf', axis=1, tiled=True)]
    dot_general x4 -> x0, matrix products: 45 us -> none  [weighted_sums(): jnp.einsum('ns,cs->cn', weight, term_rows, precision=lax.Precision.HIGHEST)]
    pallas_call x0 -> x3, Pallas kernels: none -> 23.6 us  [the longest x1 20.4 us: shards(): pl.pallas_call(sums_kernel, out_shape=(jax.ShapeDtypeStruct((SIDE, 8, 2 *...]
    all_to_all x0 -> x2, blocking collectives: none -> 21.8 us  [the longest x1 11.4 us: shards(): received = lax.all_to_all(partial, 'y', 0, 0)]
    all_to_all x0 -> x1, waiting for transfers between devices: none -> 13.3 us  [shards(): surfaces = lax.all_to_all(message, 'z', 0, 0)]
    ppermute x2 -> x1, starting transfers between devices: 9.78 us -> 21.3 us  [shards(): outer = lax.ppermute(lent[:3], ('vol', 'z', 'y'), ends)]
    gather x3 -> x0, local copies, waits for them, and re-layouts: 6.37 us -> none  [the longest x2 5.8 us: shards(): corners = extended[:, connectivity]]
  transfers between devices with their start and end apart: 3 -> 2, of which waited for: 2 -> 2; matrix products, arithmetic and copies ran while one was open for 0% -> 0% of each run, Pallas kernels for 0% -> 0%
where the time goes in v1:
time: 89.6 us; the launch traced here: 89.2 us
  starting transfers between devices  26.6 us (30%)
  Pallas kernels  23.6 us (26%)
  blocking collectives  21.8 us (24%)
  waiting for transfers between devices  14.4 us (16%)
  local copies, waits for them, and re-layouts  2.01 us (2%)
    ppermute x1, starting transfers between devices, shards(): outer = lax.ppermute(lent[:3], ('vol', 'z', 'y'), ends)  21.3 us
    pallas_call x1, Pallas kernels, shards(): pl.pallas_call(sums_kernel, out_shape=(jax.ShapeDtypeStruct((SIDE, 8, 2 *...  20.4 us
    all_to_all x1, waiting for transfers between devices, shards(): surfaces = lax.all_to_all(message, 'z', 0, 0)  13.3 us
    all_to_all x1, blocking collectives, shards(): received = lax.all_to_all(partial, 'y', 0, 0)  11.4 us
    all_to_all x1, blocking collectives, shards(): lax.all_to_all(jnp.broadcast_to(own[None], (SIDE, 8, nodes)), 'y', 0, 0)  10.4 us
    all_to_all x1, starting transfers between devices, shards(): surfaces = lax.all_to_all(message, 'z', 0, 0)  5.26 us
  transfers between devices with their start and end apart: 2, of which 2 were waited for; matrix products, arithmetic and copies ran while one was open for 0% of the time, Pallas kernels for 0%

profile of v1, /device:TPU:14, one launch (start us, length us, event | category | flops | bytes accessed | tf_op | source)
XLA Modules:
  0.0 89.2 jit_solution(12485671897530765717)
XLA Ops:
  0.6 0.0 copy-start.2
  0.6 0.6 copy-done.2
  1.3 0.6 pad.4.halo
  1.9 1.5 %shard_map.77 = (f32[8,8,1152]{2,1,0:T(8,128)}, f32[8,128]{1,0:T(8,128)}) custom-call(f32[3,128]{1,0:T(4,128)} %points.1, f32[3,1024]{1,0:T(4,128)} %surface.1, f32[3,1024]{1,0:T(4,128)} %displacement.1, f32[3,1024]{1,0:T(4,128)} %rotation.1, s32[8,128]{1,0:T(8,128)} %pad.4.halo), custom_call_target="tpu_custom_call" | custom-call | tf_op jit(solution)/shard_map/pallas_call | solution.py:171
  3.4 0.7 slice.6
  4.1 21.3 %collective-permute-start = (f32[3,128]{1,0:T(4,128)S(1)}, f32[3,128]{1,0:T(4,128)S(1)}, u32[]{:S(2)}, u32[]{:S(2)}) collective-permute-start(f32[3,128]{1,0:T(4,128)S(1)} %slice.6), channel_id=1, source_target_pairs={{7,8},{8,7},{15,16},{16,15},{23,24},{24,23},{31,32},{32,31},{39,40... | collective-permute-start | bytes 4616 | tf_op jit(solution)/shard_map/ppermute | solution.py:182
  25.4 0.0 copy-start.1
  25.4 0.1 pad.7.clone
  25.5 1.2 %collective-permute-done = f32[3,128]{1,0:T(4,128)S(1)} collective-permute-done((f32[3,128]{1,0:T(4,128)S(1)}, f32[3,128]{1,0:T(4,128)S(1)}, u32[]{:S(2)}, u32[]{:S(2)}) %collective-permute-start) | collective-permute-done | bytes 1568 | tf_op jit(solution)/shard_map/ppermute | solution.py:182
  26.7 0.0 copy-done.1
  26.7 0.1 pad_maximum_fusion
  26.8 10.4 %all_to_all.15.nodes = f32[8,8,128]{2,1,0:T(8,128)S(1)} all-to-all(f32[8,8,128]{2,1,0:T(8,128)S(1)} %broadcast_in_dim.14), channel_id=1, replica_groups=mesh['vol'=16,'z'=8,'y'=8] {'y'}, dimensions={0} | all-to-all | bytes 65536 | tf_op jit(solution)/shard_map/all_to_all | solution.py:187
  37.2 5.3 %all-to-all-start.1 = ((f32[8,8,1152]{2,1,0:T(8,128)}), f32[8,8,1152]{2,1,0:T(8,128)S(1)}, u32[]{:S(2)}, u32[]{:S(2)}) async-start(f32[8,8,1152]{2,1,0:T(8,128)} %get-tuple-element.9), calls=%async_computation.1 | async-start | bytes 589824 | tf_op jit(solution)/shard_map/all_to_all | solution.py:183
  42.4 13.3 %all-to-all-done.1.surface = f32[8,8,1152]{2,1,0:T(8,128)S(1)} async-done(((f32[8,8,1152]{2,1,0:T(8,128)}), f32[8,8,1152]{2,1,0:T(8,128)S(1)}, u32[]{:S(2)}, u32[]{:S(2)}) %all-to-all-start.1) | async-done | bytes 294944 | tf_op jit(solution)/shard_map/all_to_all | solution.py:183
  55.7 20.4 %shard_map.78 = (f32[8,8,256]{2,1,0:T(8,128)S(1)}, f32[8,256]{1,0:T(8,128)S(1)}) custom-call(s32[1]{0:T(128)} %bitcast.place, f32[8,8,128]{2,1,0:T(8,128)S(1)} %all_to_all.15.nodes, f32[8,8,1152]{2,1,0:T(8,128)S(1)} %all-to-all-done.1.surface), custom_call_target="tpu_custom_call" | custom-call | tf_op jit(solution)/shard_map/pallas_call | solution.py:190
  76.1 0.0 copy-start
  76.1 11.4 %all_to_all.16.received = f32[8,8,256]{2,1,0:T(8,128)} all-to-all(f32[8,8,256]{2,1,0:T(8,128)S(1)} %get-tuple-element.10), channel_id=1, replica_groups=mesh['vol'=16,'z'=8,'y'=8] {'y'}, dimensions={0} | all-to-all | bytes 131072 | tf_op jit(solution)/shard_map/all_to_all | solution.py:208
  87.5 0.0 copy-done
  87.5 1.6 %shard_map.79 = (f32[3,128]{1,0:T(4,128)}, f32[4,128]{1,0:T(4,128)}) custom-call(f32[8,8,256]{2,1,0:T(8,128)} %all_to_all.16.received, f32[8,256]{1,0:T(8,128)} %copy-done, s32[4,512]{1,0:T(4,128)} %cells.1), custom_call_target="tpu_custom_call" | custom-call | tf_op jit(solution)/shard_map/pallas_call | solution.py:210
  (2 shorter events, 0.0 us)
Async XLA Ops:
  0.6 0.7 copy-start.2
  4.1 22.6 %collective-permute-start = (f32[3,128]{1,0:T(4,128)S(1)}, f32[3,128]{1,0:T(4,128)S(1)}, u32[]{:S(2)}, u32[]{:S(2)}) collective-permute-start(f32[3,128]{1,0:T(4,128)S(1)} %slice.6), channel_id=1, source_target_pairs={{7,8},{8,7},{15,16},{16,15},{23,24},{24,23},{31,32},{32,31},{39,40... | collective-permute-start | bytes 4616 | tf_op jit(solution)/shard_map/ppermute | solution.py:182
  25.4 1.3 %copy-start.1 = (f32[3,128]{1,0:T(4,128)S(1)}, f32[3,128]{1,0:T(4,128)}, u32[]{:S(2)}) copy-start(f32[3,128]{1,0:T(4,128)} %points.1) | copy-start | bytes 4612
  37.2 18.5 %all-to-all-start.1 = ((f32[8,8,1152]{2,1,0:T(8,128)}), f32[8,8,1152]{2,1,0:T(8,128)S(1)}, u32[]{:S(2)}, u32[]{:S(2)}) async-start(f32[8,8,1152]{2,1,0:T(8,128)} %get-tuple-element.9), calls=%async_computation.1 | async-start | bytes 589824 | tf_op jit(solution)/shard_map/all_to_all | solution.py:183
  76.1 11.4 %copy-start = (f32[8,256]{1,0:T(8,128)}, f32[8,256]{1,0:T(8,128)S(1)}, u32[]{:S(2)}) copy-start(f32[8,256]{1,0:T(8,128)S(1)} %get-tuple-element.11.near) | copy-start | bytes 24580

commit v2 on v1

v2 whole, which is shorter than its diff:
```python
import jax
import jax.numpy as jnp
from jax import lax
from jax.experimental import pallas as pl
from jax.experimental.pallas import tpu as pltpu
from jax.sharding import Mesh
from jax.sharding import PartitionSpec as P

SOFTENING = 0.01
F32 = jnp.float32
BF16 = jnp.bfloat16
SIDE = 8
LANES = 128
OWN_STEP = 2048
SURF_STEP = 2048


def rows_of(shape):
    return lax.broadcasted_iota(jnp.int32, shape, 0)


def lanes_of(shape):
    return lax.broadcasted_iota(jnp.int32, shape, 1)


def cross3(a, b):
    return (
        a[1] * b[2] - a[2] * b[1],
        a[2] * b[0] - a[0] * b[2],
        a[0] * b[1] - a[1] * b[0],
    )


def in_three(value):
    high = value.astype(BF16).astype(F32)
    rest = value - high
    middle = rest.astype(BF16).astype(F32)
    return high, middle, rest - middle


def pick_lanes(table, index):
    spread = jnp.broadcast_to(index, table.shape)
    return jnp.take_along_axis(table, spread, axis=1, mode="promise_in_bounds")


def prepare_kernel(points, surface, displacement, rotation, halo, message, own, lent, index):
    at = [surface[i : i + 1, :] for i in range(3)]
    turn = [rotation[i : i + 1, :] for i in range(3)]
    rotated = cross3(turn, at)
    term = [displacement[i : i + 1, :] - rotated[i] for i in range(3)]
    body = jnp.concatenate(term + turn[:2] + at, axis=0)
    last = jnp.concatenate([turn[2][:, i * LANES : (i + 1) * LANES] for i in range(SIDE)], axis=0)
    whole = jnp.concatenate([body, last], axis=1)
    for i in range(SIDE):
        message[i] = whole
    index[...] = jnp.zeros_like(index)
    index[0:1, 0 : halo.shape[1]] = halo[...]
    place = index[0:1, :]
    own[...] = jnp.concatenate(
        [jnp.zeros((3, LANES), F32), place.astype(F32), jnp.zeros((1, LANES), F32), points[...]], axis=0
    )
    table = jnp.concatenate([points[...], jnp.zeros((5, LANES), F32)], axis=0)
    lent[...] = jnp.where(rows_of(table.shape) < 3, pick_lanes(table, place), 0.0)


def node_side(value):
    row = rows_of(value.shape)
    square = value[5:6] * value[5:6] + value[6:7] * value[6:7] + value[7:8] * value[7:8] + SOFTENING
    side = jnp.where(row >= 5, -2.0 * value, jnp.where(row == 3, 1.0, jnp.where(row == 4, square, 0.0)))
    high, middle, low = in_three(side)
    stack = [high, high, high, middle, middle, low, middle, low] + [jnp.zeros_like(high)] * 8
    return jnp.concatenate(stack, axis=0).astype(BF16)


def surface_side(value):
    row = rows_of(value.shape)
    square = value[5:6] * value[5:6] + value[6:7] * value[6:7] + value[7:8] * value[7:8]
    side = jnp.where(row >= 5, value, jnp.where(row == 3, square, jnp.where(row == 4, 1.0, 0.0)))
    high, middle, low = in_three(side)
    stack = [high, middle, low, high, middle, high, low, middle] + [jnp.zeros_like(high)] * 8
    return jnp.concatenate(stack, axis=0).T.astype(BF16)


def add_sums(right, terms, left, total, surf_step):
    def step(i, carry):
        s = pl.multiple_of(i * surf_step, LANES)
        spread = jnp.dot(right[pl.ds(s, surf_step), :], left[...], preferred_element_type=F32)
        inverse = lax.rsqrt(spread)
        weight = inverse * inverse * inverse
        high = weight.astype(BF16)
        low = (weight - high.astype(F32)).astype(BF16)
        term = terms[:, pl.ds(s, surf_step)]
        total[...] += jnp.dot(term, high, preferred_element_type=F32) + jnp.dot(
            term, low, preferred_element_type=F32
        )
        return carry

    total[...] = jnp.zeros_like(total)
    lax.fori_loop(0, right.shape[0] // surf_step, step, 0)


def own_kernel(own, surface, right, terms, sums, left, total):
    width = surface.shape[2] - LANES
    line = rows_of((SIDE, width))
    for part in range(SIDE):
        value = surface[part][:, :width]
        tail = surface[part][:, width:]
        tail = jnp.concatenate([tail[i : i + 1] for i in range(SIDE)], axis=1)
        right[part * width : (part + 1) * width, :] = surface_side(value)
        term = jnp.where(line < 5, value, jnp.where(line == 5, tail, jnp.where(line == 6, 1.0, 0.0)))
        high, middle, _ = in_three(term)
        terms[:, part * width : (part + 1) * width] = jnp.concatenate([high, middle], axis=0).astype(BF16)
    left[...] = node_side(own[...])
    add_sums(right, terms, left, total, OWN_STEP)
    sums[...] = total[:SIDE] + total[SIDE:]


def sums_kernel(place, nodes, right, terms, own_sums, message, near, left, total, sums, spots):
    lane = lanes_of((SIDE, LANES))
    here = place[0]
    outer = jnp.where(lane < 32, nodes[0], pltpu.roll(nodes[SIDE - 1], 32, axis=1))
    outer = pltpu.roll(outer, 5, axis=0)
    for k in range(SIDE):
        value = nodes[(here + k + 1) % SIDE] if k < SIDE - 1 else outer
        left[:, k * LANES : (k + 1) * LANES] = node_side(value)
    add_sums(right, terms, left, total, SURF_STEP)
    whole = total[:SIDE] + total[SIDE:]

    def keep(block, value):
        message[block, :, :LANES] = value
        index = nodes[block][3:4].astype(jnp.int32)
        sums[block + 1] = pick_lanes(value, index)
        spots[block + 1] = pick_lanes(nodes[block], index)

    keep(here, own_sums[...])
    for k in range(SIDE - 1):
        keep((here + k + 1) % SIDE, whole[:, k * LANES : (k + 1) * LANES])
    value = whole[:, (SIDE - 1) * LANES :]
    sums[0] = value
    sums[SIDE + 1] = pltpu.roll(value, LANES - 32, axis=1)
    spots[0] = outer
    spots[SIDE + 1] = pltpu.roll(outer, LANES - 32, axis=1)
    for block in range(SIDE):
        message[block, :, LANES:] = jnp.where(lane < 32, sums[block], pltpu.roll(sums[block + 2], 32, axis=1))
    near[:, :LANES] = nodes[here]
    near[:, LANES:] = jnp.where(lane < 32, spots[here], pltpu.roll(spots[here + 2], 32, axis=1))


def swept_kernel(received, near, cells, motion_out, swept_out):
    total = received[0]
    for i in range(1, SIDE):
        total = total + received[i]
    top = [total[i : i + 1] for i in range(3)]
    turn = [total[i : i + 1] for i in range(3, 6)]
    spot = [near[i : i + 1, :] for i in range(5, 8)]
    turned = cross3(turn, spot)
    motion = [(top[i] + turned[i]) / total[6:7] for i in range(3)]
    motion_out[...] = jnp.concatenate([m[:, :LANES] for m in motion], axis=0)
    table = jnp.concatenate(spot + motion + [jnp.zeros_like(spot[0])] * 2, axis=0)
    own, lent = table[:, :LANES], table[:, LANES:]
    count = cells.shape[1]
    for group in range(count // LANES):
        corner = []
        for a in range(4):
            index = cells[a : a + 1, group * LANES : (group + 1) * LANES]
            inside = (index >= 32) & (index < 160)
            from_own = pick_lanes(own, jnp.where(inside, index - 32, 0))
            from_lent = pick_lanes(lent, jnp.where(inside, 0, jnp.where(index < 32, index, index - 128)))
            corner.append(jnp.where(jnp.broadcast_to(inside, own.shape), from_own, from_lent))
        move = [[c[3 + i : 4 + i] for i in range(3)] for c in corner]
        half = [[c[i : i + 1] + 0.5 * c[3 + i : 4 + i] for i in range(3)] for c in corner]
        result = jnp.zeros((1, LANES), F32)
        for p, q, r in ((1, 2, 3), (0, 3, 2), (0, 1, 3), (0, 2, 1)):
            one = [half[q][i] - half[p][i] for i in range(3)]
            two = [half[r][i] - half[p][i] for i in range(3)]
            normal = cross3(one, two)
            for i in range(3):
                average = (move[p][i] + move[q][i] + move[r][i]) / 3.0
                result = result + average * (0.5 * normal[i])
        swept_out[group : group + 1, :] = result


def shards(points, surface, displacement, rotation, halo_index, connectivity):
    width = surface.shape[1]
    nodes = points.shape[1]
    lend = halo_index.shape[0]
    message, own, lent = pl.pallas_call(
        prepare_kernel,
        out_shape=(
            jax.ShapeDtypeStruct((SIDE, 8, width + LANES), F32),
            jax.ShapeDtypeStruct((8, LANES), F32),
            jax.ShapeDtypeStruct((8, LANES), F32),
        ),
        scratch_shapes=[pltpu.VMEM((8, LANES), jnp.int32)],
    )(points, surface, displacement, rotation, halo_index.reshape(1, lend))
    blocks = lax.axis_size("vol") * SIDE * SIDE
    ends = []
    for b in range(SIDE - 1, blocks, SIDE):
        ends += [(b, (b + 1) % blocks), ((b + 1) % blocks, b)]
    outer = lax.ppermute(lent, ("vol", "z", "y"), ends)
    surfaces = lax.all_to_all(message, "z", 0, 0)
    surfaces, own, outer = lax.optimization_barrier((surfaces, own, outer))
    repeated = jnp.broadcast_to((own + outer)[None], (SIDE, 8, nodes))
    around = lax.all_to_all(repeated, "y", 0, 0)
    total_surface = SIDE * width
    right, terms, own_sums = pl.pallas_call(
        own_kernel,
        out_shape=(
            jax.ShapeDtypeStruct((total_surface, LANES), BF16),
            jax.ShapeDtypeStruct((16, total_surface), BF16),
            jax.ShapeDtypeStruct((8, LANES), F32),
        ),
        scratch_shapes=[pltpu.VMEM((LANES, LANES), BF16), pltpu.VMEM((16, LANES), F32)],
        compiler_params=pltpu.CompilerParams(vmem_limit_bytes=24 << 20),
        cost_estimate=pl.CostEstimate(flops=5 * 10**9, bytes_accessed=3 << 20, transcendentals=1 << 20),
    )(own, surfaces)
    place = lax.axis_index("y").astype(jnp.int32).reshape(1)
    vmem = pl.BlockSpec(memory_space=pltpu.VMEM)
    partial, near = pl.pallas_call(
        sums_kernel,
        out_shape=(
            jax.ShapeDtypeStruct((SIDE, 8, 2 * LANES), F32),
            jax.ShapeDtypeStruct((8, 2 * LANES), F32),
        ),
        in_specs=[pl.BlockSpec(memory_space=pltpu.SMEM), vmem, vmem, vmem, vmem],
        out_specs=(vmem, vmem),
        scratch_shapes=[
            pltpu.VMEM((LANES, SIDE * LANES), BF16),
            pltpu.VMEM((16, SIDE * LANES), F32),
            pltpu.VMEM((SIDE + 2, 8, LANES), F32),
            pltpu.VMEM((SIDE + 2, 8, LANES), F32),
        ],
        compiler_params=pltpu.CompilerParams(vmem_limit_bytes=40 << 20),
        cost_estimate=pl.CostEstimate(flops=30 * 10**9, bytes_accessed=3 << 20, transcendentals=8 << 20),
    )(place, around, right, terms, own_sums)
    received = lax.all_to_all(partial, "y", 0, 0)
    count = connectivity.shape[1]
    motion, swept = pl.pallas_call(
        swept_kernel,
        out_shape=(
            jax.ShapeDtypeStruct((3, nodes), F32),
            jax.ShapeDtypeStruct((count // LANES, LANES), F32),
        ),
    )(received, near, connectivity)
    return motion, swept.reshape(count)


def solution(mesh):
    split = Mesh(mesh.devices.reshape(mesh.devices.shape[0], SIDE, SIDE), ("vol", "z", "y"))
    nodes = ("vol", "z", "y")
    surface = P(None, ("z", "y"))
    in_specs = (P(None, nodes), surface, surface, surface, P(nodes), P(None, nodes))
    out_specs = (P(None, nodes), P(nodes))
    return jax.shard_map(shards, mesh=split, in_specs=in_specs, out_specs=out_specs, check_vma=False)
```

time: 89.6 us -> 72.6 us (0.81)
  blocking collectives: 21.8 us -> 11.5 us
  Pallas kernels: 23.6 us -> 17.1 us
  waiting for transfers between devices: 14.4 us -> 8.11 us
  starting transfers between devices: 26.6 us -> 32.7 us
    ppermute x1, starting transfers between devices: 21.3 us -> 8.58 us  [shards(): outer = lax.ppermute(lent, ('vol', 'z', 'y'), ends)]
    all_to_all x1, starting transfers between devices: 5.26 us -> 16.7 us  [shards(): surfaces = lax.all_to_all(message, 'z', 0, 0)]
    all_to_all x1, waiting for transfers between devices: 13.3 us -> 2.56 us  [shards(): surfaces = lax.all_to_all(message, 'z', 0, 0)]
    all_to_all x1 -> x0, blocking collectives: 10.4 us -> none  [shards(): lax.all_to_all(jnp.broadcast_to(own[None], (SIDE, 8, nodes)), 'y', 0, 0)]
    pallas_call x1, Pallas kernels: 20.4 us -> 10.7 us  [shards(): pl.pallas_call(sums_kernel, out_shape=(jax.ShapeDtypeStruct((SIDE, 8, 2 *...]
    all_to_all x0 -> x1, starting transfers between devices: none -> 7.47 us  [shards(): around = lax.all_to_all(repeated, 'y', 0, 0)]
    all_to_all x0 -> x1, waiting for transfers between devices: none -> 4.04 us  [shards(): around = lax.all_to_all(repeated, 'y', 0, 0)]
    pallas_call x0 -> x1, Pallas kernels: none -> 3.31 us  [shards(): pl.pallas_call(own_kernel, out_shape=(jax.ShapeDtypeStruct((total_surface...]
  transfers between devices with their start and end apart: 2 -> 3, of which waited for: 2 -> 3; matrix products, arithmetic and copies ran while one was open for 0% -> 0% of each run, Pallas kernels for 0% -> 5%
where the time goes in v2:
time: 72.6 us; the launch traced here: 72.1 us
  starting transfers between devices  32.7 us (45%)
  Pallas kernels  17.1 us (24%)
  blocking collectives  11.5 us (16%)
  waiting for transfers between devices  8.11 us (11%)
  local copies, waits for them, and re-layouts  1.31 us (2%)
    all_to_all x1, starting transfers between devices, shards(): surfaces = lax.all_to_all(message, 'z', 0, 0)  16.7 us
    all_to_all x1, blocking collectives, shards(): received = lax.all_to_all(partial, 'y', 0, 0)  11.5 us
    pallas_call x1, Pallas kernels, shards(): pl.pallas_call(sums_kernel, out_shape=(jax.ShapeDtypeStruct((SIDE, 8, 2 *...  10.7 us
    ppermute x1, starting transfers between devices, shards(): outer = lax.ppermute(lent, ('vol', 'z', 'y'), ends)  8.58 us
    all_to_all x1, starting transfers between devices, shards(): around = lax.all_to_all(repeated, 'y', 0, 0)  7.47 us
    all_to_all x1, waiting for transfers between devices, shards(): around = lax.all_to_all(repeated, 'y', 0, 0)  4.04 us
    pallas_call x1, Pallas kernels, shards(): pl.pallas_call(own_kernel, out_shape=(jax.ShapeDtypeStruct((total_surface...  3.31 us
    all_to_all x1, waiting for transfers between devices, shards(): surfaces = lax.all_to_all(message, 'z', 0, 0)  2.56 us
  transfers between devices with their start and end apart: 3, of which 3 were waited for; matrix products, arithmetic and copies ran while one was open for 0% of the time, Pallas kernels for 5%

profile of v2, /device:TPU:14, one launch (start us, length us, event | category | flops | bytes accessed | tf_op | source)
XLA Modules:
  0.0 72.1 jit_solution(9656116499360721308)
XLA Ops:
  0.6 1.5 %shard_map.77 = (f32[8,8,1152]{2,1,0:T(8,128)}, f32[8,128]{1,0:T(8,128)}, f32[8,128]{1,0:T(8,128)}) custom-call(f32[3,128]{1,0:T(4,128)} %points.1, f32[3,1024]{1,0:T(4,128)} %surface.1, f32[3,1024]{1,0:T(4,128)} %displacement.1, f32[3,1024]{1,0:T(4,128)} %rotation.1, s32[1,32]{1,0:T(1,128)} %bitcast.3), custom_call_target="tpu_custom_call" | custom-call | tf_op jit(solution)/shard_map/pallas_call | solution.py:187
  2.2 16.7 %all-to-all-start = ((f32[8,8,1152]{2,1,0:T(8,128)}), f32[8,8,1152]{2,1,0:T(8,128)S(1)}, u32[]{:S(2)}, u32[]{:S(2)}) async-start(f32[8,8,1152]{2,1,0:T(8,128)} %get-tuple-element.15), calls=%async_computation | async-start | bytes 589824 | tf_op jit(solution)/shard_map/all_to_all | solution.py:201
  18.9 8.6 %collective-permute-start = (f32[8,128]{1,0:T(8,128)}, f32[8,128]{1,0:T(8,128)S(1)}, u32[]{:S(2)}, u32[]{:S(2)}) collective-permute-start(f32[8,128]{1,0:T(8,128)} %get-tuple-element.17), channel_id=1, source_target_pairs={{7,8},{8,7},{15,16},{16,15},{23,24},{24,23},{31,32},{32,31},{39,40... | collective-permute-start | bytes 12296 | tf_op jit(solution)/shard_map/ppermute | solution.py:200
  27.4 1.5 %collective-permute-done = f32[8,128]{1,0:T(8,128)S(1)} collective-permute-done((f32[8,128]{1,0:T(8,128)}, f32[8,128]{1,0:T(8,128)S(1)}, u32[]{:S(2)}, u32[]{:S(2)}) %collective-permute-start) | collective-permute-done | bytes 4128 | tf_op jit(solution)/shard_map/ppermute | solution.py:200
  29.0 2.6 %all-to-all-done.surface = f32[8,8,1152]{2,1,0:T(8,128)S(1)} async-done(((f32[8,8,1152]{2,1,0:T(8,128)}), f32[8,8,1152]{2,1,0:T(8,128)S(1)}, u32[]{:S(2)}, u32[]{:S(2)}) %all-to-all-start) | async-done | bytes 294944 | tf_op jit(solution)/shard_map/all_to_all | solution.py:201
  31.5 0.7 add.3
  32.2 0.6 broadcast_in_dim.2
  32.8 7.5 %all-to-all-start.1 = ((f32[8,8,128]{2,1,0:T(8,128)}), f32[8,8,128]{2,1,0:T(8,128)S(1)}, u32[]{:S(2)}, u32[]{:S(2)}) async-start(f32[8,8,128]{2,1,0:T(8,128)} %broadcast_in_dim.2), calls=%async_computation.1 | async-start | bytes 65536 | tf_op jit(solution)/shard_map/all_to_all | solution.py:204
  40.3 0.0 copy-start.1
  40.3 0.7 copy-done.1
  41.0 3.3 %shard_map.78 = (bf16[8192,128]{1,0:T(8,128)(2,1)S(1)}, bf16[16,8192]{1,0:T(8,128)(2,1)S(1)}, f32[8,128]{1,0:T(8,128)S(1)}) custom-call(f32[8,128]{1,0:T(8,128)S(1)} %copy-done.1, f32[8,8,1152]{2,1,0:T(8,128)S(1)} %all-to-all-done.surface), custom_call_target="tpu_custom_call" | custom-call | flops 5000000000 | bytes 3145728 | tf_op jit(solution)/shard_map/pallas_call | solution.py:206
  44.3 4.0 %all-to-all-done.1.nodes = f32[8,8,128]{2,1,0:T(8,128)S(1)} async-done(((f32[8,8,128]{2,1,0:T(8,128)}), f32[8,8,128]{2,1,0:T(8,128)S(1)}, u32[]{:S(2)}, u32[]{:S(2)}) %all-to-all-start.1) | async-done | bytes 32800 | tf_op jit(solution)/shard_map/all_to_all | solution.py:204
  48.3 10.7 %shard_map.79 = (f32[8,8,256]{2,1,0:T(8,128)S(1)}, f32[8,256]{1,0:T(8,128)S(1)}) custom-call(s32[1]{0:T(128)} %bitcast.place, f32[8,8,128]{2,1,0:T(8,128)S(1)} %all-to-all-done.1.nodes, bf16[8192,128]{1,0:T(8,128)(2,1)S(1)} %get-tuple-element.21.right, bf16[16,8192]{1,0:T(8,128)(2,1)S(1)} %get-tuple-element.22.terms, f32[8,128]{1,0:T(8,128)S(1)} %get-tuple-element.23.own_sums), custom_call_target="tpu_custom_call" | custom-call | flops 30000001024 | bytes 3145728 | tf_op jit(solution)/shard_map/pallas_call | solution.py:219
  59.0 0.0 copy-start
  59.0 11.5 %all_to_all.15.received = f32[8,8,256]{2,1,0:T(8,128)} all-to-all(f32[8,8,256]{2,1,0:T(8,128)S(1)} %get-tuple-element.24), channel_id=1, replica_groups=mesh['vol'=16,'z'=8,'y'=8] {'y'}, dimensions={0} | all-to-all | bytes 131072 | tf_op jit(solution)/shard_map/all_to_all | solution.py:236
  70.5 0.0 copy-done
  70.5 1.6 %shard_map.80 = (f32[3,128]{1,0:T(4,128)}, f32[4,128]{1,0:T(4,128)}) custom-call(f32[8,8,256]{2,1,0:T(8,128)} %all_to_all.15.received, f32[8,256]{1,0:T(8,128)} %copy-done, s32[4,512]{1,0:T(4,128)} %cells.1), custom_call_target="tpu_custom_call" | custom-call | tf_op jit(solution)/shard_map/pallas_call | solution.py:238
Async XLA Ops:
  2.2 29.3 %all-to-all-start = ((f32[8,8,1152]{2,1,0:T(8,128)}), f32[8,8,1152]{2,1,0:T(8,128)S(1)}, u32[]{:S(2)}, u32[]{:S(2)}) async-start(f32[8,8,1152]{2,1,0:T(8,128)} %get-tuple-element.15), calls=%async_computation | async-start | bytes 589824 | tf_op jit(solution)/shard_map/all_to_all | solution.py:201
  18.9 10.1 %collective-permute-start = (f32[8,128]{1,0:T(8,128)}, f32[8,128]{1,0:T(8,128)S(1)}, u32[]{:S(2)}, u32[]{:S(2)}) collective-permute-start(f32[8,128]{1,0:T(8,128)} %get-tuple-element.17), channel_id=1, source_target_pairs={{7,8},{8,7},{15,16},{16,15},{23,24},{24,23},{31,32},{32,31},{39,40... | collective-permute-start | bytes 12296 | tf_op jit(solution)/shard_map/ppermute | solution.py:200
  32.8 15.5 %all-to-all-start.1 = ((f32[8,8,128]{2,1,0:T(8,128)}), f32[8,8,128]{2,1,0:T(8,128)S(1)}, u32[]{:S(2)}, u32[]{:S(2)}) async-start(f32[8,8,128]{2,1,0:T(8,128)} %broadcast_in_dim.2), calls=%async_computation.1 | async-start | bytes 65536 | tf_op jit(solution)/shard_map/all_to_all | solution.py:204
  40.3 0.7 copy-start.1
  59.0 11.5 %copy-start = (f32[8,256]{1,0:T(8,128)}, f32[8,256]{1,0:T(8,128)S(1)}, u32[]{:S(2)}) copy-start(f32[8,256]{1,0:T(8,128)S(1)} %get-tuple-element.25.near) | copy-start | bytes 24580

commit v3 on v2

--- a/solution.py
+++ b/solution.py
@@ -12,7 +12,7 @@
 SIDE = 8
 LANES = 128
 OWN_STEP = 2048
-SURF_STEP = 2048
+SURF_STEP = 4096
 
 
 def rows_of(shape):
@@ -56,9 +56,11 @@
     index[...] = jnp.zeros_like(index)
     index[0:1, 0 : halo.shape[1]] = halo[...]
     place = index[0:1, :]
-    own[...] = jnp.concatenate(
+    mine = jnp.concatenate(
         [jnp.zeros((3, LANES), F32), place.astype(F32), jnp.zeros((1, LANES), F32), points[...]], axis=0
     )
+    for i in range(SIDE):
+        own[i] = mine
     table = jnp.concatenate([points[...], jnp.zeros((5, LANES), F32)], axis=0)
     lent[...] = jnp.where(rows_of(table.shape) < 3, pick_lanes(table, place), 0.0)
 
@@ -99,7 +101,7 @@
     lax.fori_loop(0, right.shape[0] // surf_step, step, 0)
 
 
-def own_kernel(own, surface, right, terms, sums, left, total):
+def own_kernel(points, surface, right, terms, sums, left, total):
     width = surface.shape[2] - LANES
     line = rows_of((SIDE, width))
     for part in range(SIDE):
@@ -110,7 +112,7 @@
         term = jnp.where(line < 5, value, jnp.where(line == 5, tail, jnp.where(line == 6, 1.0, 0.0)))
         high, middle, _ = in_three(term)
         terms[:, part * width : (part + 1) * width] = jnp.concatenate([high, middle], axis=0).astype(BF16)
-    left[...] = node_side(own[...])
+    left[...] = node_side(jnp.concatenate([jnp.zeros((5, LANES), F32), points[...]], axis=0))
     add_sums(right, terms, left, total, OWN_STEP)
     sums[...] = total[:SIDE] + total[SIDE:]
 
@@ -118,7 +120,7 @@
 def sums_kernel(place, nodes, right, terms, own_sums, message, near, left, total, sums, spots):
     lane = lanes_of((SIDE, LANES))
     here = place[0]
-    outer = jnp.where(lane < 32, nodes[0], pltpu.roll(nodes[SIDE - 1], 32, axis=1))
+    outer = jnp.where(lane < 32, nodes[SIDE - 1], pltpu.roll(nodes[0], 32, axis=1))
     outer = pltpu.roll(outer, 5, axis=0)
     for k in range(SIDE):
         value = nodes[(here + k + 1) % SIDE] if k < SIDE - 1 else outer
@@ -188,20 +190,20 @@
         prepare_kernel,
         out_shape=(
             jax.ShapeDtypeStruct((SIDE, 8, width + LANES), F32),
-            jax.ShapeDtypeStruct((8, LANES), F32),
+            jax.ShapeDtypeStruct((SIDE, 8, LANES), F32),
             jax.ShapeDtypeStruct((8, LANES), F32),
         ),
         scratch_shapes=[pltpu.VMEM((8, LANES), jnp.int32)],
     )(points, surface, displacement, rotation, halo_index.reshape(1, lend))
-    blocks = lax.axis_size("vol") * SIDE * SIDE
+    rows = lax.axis_size("vol") * SIDE
     ends = []
-    for b in range(SIDE - 1, blocks, SIDE):
-        ends += [(b, (b + 1) % blocks), ((b + 1) % blocks, b)]
+    for row in range(rows):
+        after = (row + 1) % rows
+        ends += [(row * SIDE + SIDE - 1, after * SIDE + SIDE - 1), (after * SIDE, row * SIDE)]
     outer = lax.ppermute(lent, ("vol", "z", "y"), ends)
     surfaces = lax.all_to_all(message, "z", 0, 0)
     surfaces, own, outer = lax.optimization_barrier((surfaces, own, outer))
-    repeated = jnp.broadcast_to((own + outer)[None], (SIDE, 8, nodes))
-    around = lax.all_to_all(repeated, "y", 0, 0)
+    around = lax.all_to_all(own + outer, "y", 0, 0)
     total_surface = SIDE * width
     right, terms, own_sums = pl.pallas_call(
         own_kernel,
@@ -213,7 +215,7 @@
         scratch_shapes=[pltpu.VMEM((LANES, LANES), BF16), pltpu.VMEM((16, LANES), F32)],
         compiler_params=pltpu.CompilerParams(vmem_limit_bytes=24 << 20),
         cost_estimate=pl.CostEstimate(flops=5 * 10**9, bytes_accessed=3 << 20, transcendentals=1 << 20),
-    )(own, surfaces)
+    )(points, surfaces)
     place = lax.axis_index("y").astype(jnp.int32).reshape(1)
     vmem = pl.BlockSpec(memory_space=pltpu.VMEM)
     partial, near = pl.pallas_call(
@@ -241,6 +243,7 @@
             jax.ShapeDtypeStruct((3, nodes), F32),
             jax.ShapeDtypeStruct((count // LANES, LANES), F32),
         ),
+        compiler_params=pltpu.CompilerParams(vmem_limit_bytes=8 << 20),
     )(received, near, connectivity)
     return motion, swept.reshape(count)
 

time: 72.6 us -> 71.4 us (0.983)
  starting transfers between devices: 32.7 us -> 29.1 us
  waiting for transfers between devices: 8.11 us -> 11.7 us
  Pallas kernels: 17.1 us -> 15.9 us
    ppermute x1, starting transfers between devices: 8.58 us -> 4.88 us  [shards(): outer = lax.ppermute(lent, ('vol', 'z', 'y'), ends)]
    ppermute x1, waiting for transfers between devices: 1.51 us -> 3.87 us  [shards(): outer = lax.ppermute(lent, ('vol', 'z', 'y'), ends)]
    all_to_all x1, waiting for transfers between devices: 2.56 us -> 3.82 us  [shards(): surfaces = lax.all_to_all(message, 'z', 0, 0)]
    pallas_call x1, Pallas kernels: 1.64 us -> 0.79 us  [shards(): pl.pallas_call(swept_kernel, out_shape=(jax.ShapeDtypeStruct((3, nodes),...]
where the time goes in v3:
time: 71.4 us; the launch traced here: 70.9 us
  starting transfers between devices  29.1 us (41%)
  Pallas kernels  15.9 us (22%)
  waiting for transfers between devices  11.7 us (16%)
  blocking collectives  11.4 us (16%)
  other arithmetic  1.38 us (2%)
    all_to_all x1, starting transfers between devices, shards(): surfaces = lax.all_to_all(message, 'z', 0, 0)  16.7 us
    all_to_all x1, blocking collectives, shards(): received = lax.all_to_all(partial, 'y', 0, 0)  11.4 us
    pallas_call x1, Pallas kernels, shards(): pl.pallas_call(sums_kernel, out_shape=(jax.ShapeDtypeStruct((SIDE, 8, 2 *...  10.3 us
    all_to_all x1, starting transfers between devices, shards(): around = lax.all_to_all(own + outer, 'y', 0, 0)  7.56 us
    ppermute x1, starting transfers between devices, shards(): outer = lax.ppermute(lent, ('vol', 'z', 'y'), ends)  4.88 us
    all_to_all x1, waiting for transfers between devices, shards(): around = lax.all_to_all(own + outer, 'y', 0, 0)  4.03 us
    ppermute x1, waiting for transfers between devices, shards(): outer = lax.ppermute(lent, ('vol', 'z', 'y'), ends)  3.87 us
    all_to_all x1, waiting for transfers between devices, shards(): surfaces = lax.all_to_all(message, 'z', 0, 0)  3.82 us
  transfers between devices with their start and end apart: 3, of which 3 were waited for; matrix products, arithmetic and copies ran while one was open for 0% of the time, Pallas kernels for 5%

profile of v3, /device:TPU:14, one launch (start us, length us, event | category | flops | bytes accessed | tf_op | source)
XLA Modules:
  0.0 70.9 jit_solution(4356680259670715831)
XLA Ops:
  0.6 1.5 %shard_map.77 = (f32[8,8,1152]{2,1,0:T(8,128)}, f32[8,8,128]{2,1,0:T(8,128)}, f32[8,128]{1,0:T(8,128)}) custom-call(f32[3,128]{1,0:T(4,128)} %points.3, f32[3,1024]{1,0:T(4,128)} %surface.1, f32[3,1024]{1,0:T(4,128)} %displacement.1, f32[3,1024]{1,0:T(4,128)} %rotation.1, s32[1,32]{1,0:T(1,128)} %bitcast.3), custom_call_target="tpu_custom_call" | custom-call | tf_op jit(solution)/shard_map/pallas_call | solution.py:189
  2.2 16.7 %all-to-all-start = ((f32[8,8,1152]{2,1,0:T(8,128)}), f32[8,8,1152]{2,1,0:T(8,128)S(1)}, u32[]{:S(2)}, u32[]{:S(2)}) async-start(f32[8,8,1152]{2,1,0:T(8,128)} %get-tuple-element.15), calls=%async_computation | async-start | bytes 589824 | tf_op jit(solution)/shard_map/all_to_all | solution.py:204
  18.8 4.9 %collective-permute-start = (f32[8,128]{1,0:T(8,128)}, f32[8,128]{1,0:T(8,128)S(1)}, u32[]{:S(2)}, u32[]{:S(2)}) collective-permute-start(f32[8,128]{1,0:T(8,128)} %get-tuple-element.17), channel_id=1, source_target_pairs={{7,15},{8,0},{15,23},{16,8},{23,31},{24,16},{31,39},{32,24},{39,47... | collective-permute-start | bytes 12296 | tf_op jit(solution)/shard_map/ppermute | solution.py:203
  23.7 3.9 %collective-permute-done = f32[8,128]{1,0:T(8,128)S(1)} collective-permute-done((f32[8,128]{1,0:T(8,128)}, f32[8,128]{1,0:T(8,128)S(1)}, u32[]{:S(2)}, u32[]{:S(2)}) %collective-permute-start) | collective-permute-done | bytes 4128 | tf_op jit(solution)/shard_map/ppermute | solution.py:203
  27.6 3.8 %all-to-all-done.surface = f32[8,8,1152]{2,1,0:T(8,128)S(1)} async-done(((f32[8,8,1152]{2,1,0:T(8,128)}), f32[8,8,1152]{2,1,0:T(8,128)S(1)}, u32[]{:S(2)}, u32[]{:S(2)}) %all-to-all-start) | async-done | bytes 294944 | tf_op jit(solution)/shard_map/all_to_all | solution.py:204
  31.4 1.4 %broadcast_add_fusion = f32[8,8,128]{2,1,0:T(8,128)} fusion(f32[8,8,128]{2,1,0:T(8,128)} %get-tuple-element.18, f32[8,128]{1,0:T(8,128)S(1)} %collective-permute-done), kind=kLoop, calls=%fused_computation | loop fusion | flops 8192 | bytes 69632 | tf_op jit(solution)/shard_map/add | solution.py:206
  32.8 7.6 %all-to-all-start.1 = ((f32[8,8,128]{2,1,0:T(8,128)}), f32[8,8,128]{2,1,0:T(8,128)S(1)}, u32[]{:S(2)}, u32[]{:S(2)}) async-start(f32[8,8,128]{2,1,0:T(8,128)} %broadcast_add_fusion), calls=%async_computation.1 | async-start | bytes 65536 | tf_op jit(solution)/shard_map/all_to_all | solution.py:206
  40.4 0.0 copy-start.1
  40.4 0.7 copy-done.1
  41.0 3.3 %shard_map.78 = (bf16[8192,128]{1,0:T(8,128)(2,1)S(1)}, bf16[16,8192]{1,0:T(8,128)(2,1)S(1)}, f32[8,128]{1,0:T(8,128)S(1)}) custom-call(f32[3,128]{1,0:T(4,128)S(1)} %copy-done.1, f32[8,8,1152]{2,1,0:T(8,128)S(1)} %all-to-all-done.surface), custom_call_target="tpu_custom_call" | custom-call | flops 5000000000 | bytes 3145728 | tf_op jit(solution)/shard_map/pallas_call | solution.py:208
  44.4 4.0 %all-to-all-done.1.nodes = f32[8,8,128]{2,1,0:T(8,128)S(1)} async-done(((f32[8,8,128]{2,1,0:T(8,128)}), f32[8,8,128]{2,1,0:T(8,128)S(1)}, u32[]{:S(2)}, u32[]{:S(2)}) %all-to-all-start.1) | async-done | bytes 32800 | tf_op jit(solution)/shard_map/all_to_all | solution.py:206
  48.4 0.0 copy-start
  48.4 10.3 %shard_map.79 = (f32[8,8,256]{2,1,0:T(8,128)S(1)}, f32[8,256]{1,0:T(8,128)S(1)}) custom-call(s32[1]{0:T(128)} %bitcast.place, f32[8,8,128]{2,1,0:T(8,128)S(1)} %all-to-all-done.1.nodes, bf16[8192,128]{1,0:T(8,128)(2,1)S(1)} %get-tuple-element.21.right, bf16[16,8192]{1,0:T(8,128)(2,1)S(1)} %get-tuple-element.22.terms, f32[8,128]{1,0:T(8,128)S(1)} %get-tuple-element.23.own_sums), custom_call_target="tpu_custom_call" | custom-call | flops 30000001024 | bytes 3145728 | tf_op jit(solution)/shard_map/pallas_call | solution.py:221
  58.7 11.4 %all_to_all.15.received = f32[8,8,256]{2,1,0:T(8,128)S(1)} all-to-all(f32[8,8,256]{2,1,0:T(8,128)S(1)} %get-tuple-element.24), channel_id=1, replica_groups=mesh['vol'=16,'z'=8,'y'=8] {'y'}, dimensions={0} | all-to-all | bytes 131072 | tf_op jit(solution)/shard_map/all_to_all | solution.py:238
  70.1 0.0 copy-done
  70.1 0.8 %shard_map.80 = (f32[3,128]{1,0:T(4,128)}, f32[4,128]{1,0:T(4,128)}) custom-call(f32[8,8,256]{2,1,0:T(8,128)S(1)} %all_to_all.15.received, f32[8,256]{1,0:T(8,128)S(1)} %get-tuple-element.25.near, s32[4,512]{1,0:T(4,128)S(1)} %copy-done), custom_call_target="tpu_custom_call" | custom-call | tf_op jit(solution)/shard_map/pallas_call | solution.py:240
Async XLA Ops:
  2.2 29.3 %all-to-all-start = ((f32[8,8,1152]{2,1,0:T(8,128)}), f32[8,8,1152]{2,1,0:T(8,128)S(1)}, u32[]{:S(2)}, u32[]{:S(2)}) async-start(f32[8,8,1152]{2,1,0:T(8,128)} %get-tuple-element.15), calls=%async_computation | async-start | bytes 589824 | tf_op jit(solution)/shard_map/all_to_all | solution.py:204
  18.8 8.8 %collective-permute-start = (f32[8,128]{1,0:T(8,128)}, f32[8,128]{1,0:T(8,128)S(1)}, u32[]{:S(2)}, u32[]{:S(2)}) collective-permute-start(f32[8,128]{1,0:T(8,128)} %get-tuple-element.17), channel_id=1, source_target_pairs={{7,15},{8,0},{15,23},{16,8},{23,31},{24,16},{31,39},{32,24},{39,47... | collective-permute-start | bytes 12296 | tf_op jit(solution)/shard_map/ppermute | solution.py:203
  32.8 15.6 %all-to-all-start.1 = ((f32[8,8,128]{2,1,0:T(8,128)}), f32[8,8,128]{2,1,0:T(8,128)S(1)}, u32[]{:S(2)}, u32[]{:S(2)}) async-start(f32[8,8,128]{2,1,0:T(8,128)} %broadcast_add_fusion), calls=%async_computation.1 | async-start | bytes 65536 | tf_op jit(solution)/shard_map/all_to_all | solution.py:206
  40.4 0.7 copy-start.1
  48.4 21.7 %copy-start = (s32[4,512]{1,0:T(4,128)S(1)}, s32[4,512]{1,0:T(4,128)}, u32[]{:S(2)}) copy-start(s32[4,512]{1,0:T(4,128)} %cells.1) | copy-start | bytes 24580

commit v4 on v3

--- a/solution.py
+++ b/solution.py
@@ -11,7 +11,7 @@
 BF16 = jnp.bfloat16
 SIDE = 8
 LANES = 128
-OWN_STEP = 2048
+OWN_STEP = 8192
 SURF_STEP = 4096
 
 
@@ -202,8 +202,8 @@
         ends += [(row * SIDE + SIDE - 1, after * SIDE + SIDE - 1), (after * SIDE, row * SIDE)]
     outer = lax.ppermute(lent, ("vol", "z", "y"), ends)
     surfaces = lax.all_to_all(message, "z", 0, 0)
-    surfaces, own, outer = lax.optimization_barrier((surfaces, own, outer))
-    around = lax.all_to_all(own + outer, "y", 0, 0)
+    surfaces, ready = lax.optimization_barrier((surfaces, own + outer))
+    around = lax.all_to_all(ready, "y", 0, 0)
     total_surface = SIDE * width
     right, terms, own_sums = pl.pallas_call(
         own_kernel,

time: 71.4 us -> 69.4 us (0.972)
  Pallas kernels: 15.9 us -> 14.7 us
    all_to_all x1, waiting for transfers between devices: 3.82 us -> 2.45 us  [shards(): surfaces = lax.all_to_all(message, 'z', 0, 0)]
    pallas_call x1, Pallas kernels: 3.31 us -> 2.12 us  [shards(): pl.pallas_call(own_kernel, out_shape=(jax.ShapeDtypeStruct((total_surface...]
    all_to_all x1, waiting for transfers between devices: 4.03 us -> 5.22 us  [shards(): around = lax.all_to_all(ready, 'y', 0, 0)]
  transfers between devices with their start and end apart: 3 -> 3, of which waited for: 3 -> 3; matrix products, arithmetic and copies ran while one was open for 0% -> 2% of each run, Pallas kernels for 5% -> 3%
where the time goes in v4:
time: 69.4 us; the launch traced here: 68.9 us
  starting transfers between devices  29.1 us (42%)
  Pallas kernels  14.7 us (21%)
  waiting for transfers between devices  11.5 us (17%)
  blocking collectives  10.8 us (16%)
  other arithmetic  1.37 us (2%)
    all_to_all x1, starting transfers between devices, shards(): surfaces = lax.all_to_all(message, 'z', 0, 0)  16.7 us
    all_to_all x1, blocking collectives, shards(): received = lax.all_to_all(partial, 'y', 0, 0)  10.8 us
    pallas_call x1, Pallas kernels, shards(): pl.pallas_call(sums_kernel, out_shape=(jax.ShapeDtypeStruct((SIDE, 8, 2 *...  10.3 us
    all_to_all x1, starting transfers between devices, shards(): around = lax.all_to_all(ready, 'y', 0, 0)  7.56 us
    all_to_all x1, waiting for transfers between devices, shards(): around = lax.all_to_all(ready, 'y', 0, 0)  5.22 us
    ppermute x1, starting transfers between devices, shards(): outer = lax.ppermute(lent, ('vol', 'z', 'y'), ends)  4.88 us
    ppermute x1, waiting for transfers between devices, shards(): outer = lax.ppermute(lent, ('vol', 'z', 'y'), ends)  3.87 us
    all_to_all x1, waiting for transfers between devices, shards(): surfaces = lax.all_to_all(message, 'z', 0, 0)  2.45 us
  transfers between devices with their start and end apart: 3, of which 3 were waited for; matrix products, arithmetic and copies ran while one was open for 2% of the time, Pallas kernels for 3%

profile of v4, /device:TPU:14, one launch (start us, length us, event | category | flops | bytes accessed | tf_op | source)
XLA Modules:
  0.0 68.9 jit_solution(2333193718095595572)
XLA Ops:
  0.6 1.5 %shard_map.77 = (f32[8,8,1152]{2,1,0:T(8,128)}, f32[8,8,128]{2,1,0:T(8,128)}, f32[8,128]{1,0:T(8,128)}) custom-call(f32[3,128]{1,0:T(4,128)} %points.3, f32[3,1024]{1,0:T(4,128)} %surface.1, f32[3,1024]{1,0:T(4,128)} %displacement.1, f32[3,1024]{1,0:T(4,128)} %rotation.1, s32[1,32]{1,0:T(1,128)} %bitcast.3), custom_call_target="tpu_custom_call" | custom-call | tf_op jit(solution)/shard_map/pallas_call | solution.py:189
  2.2 16.7 %all-to-all-start = ((f32[8,8,1152]{2,1,0:T(8,128)}), f32[8,8,1152]{2,1,0:T(8,128)S(1)}, u32[]{:S(2)}, u32[]{:S(2)}) async-start(f32[8,8,1152]{2,1,0:T(8,128)} %get-tuple-element.14), calls=%async_computation | async-start | bytes 589824 | tf_op jit(solution)/shard_map/all_to_all | solution.py:204
  18.8 4.9 %collective-permute-start = (f32[8,128]{1,0:T(8,128)}, f32[8,128]{1,0:T(8,128)S(1)}, u32[]{:S(2)}, u32[]{:S(2)}) collective-permute-start(f32[8,128]{1,0:T(8,128)} %get-tuple-element.16), channel_id=1, source_target_pairs={{7,15},{8,0},{15,23},{16,8},{23,31},{24,16},{31,39},{32,24},{39,47... | collective-permute-start | bytes 12296 | tf_op jit(solution)/shard_map/ppermute | solution.py:203
  23.7 3.9 %collective-permute-done = f32[8,128]{1,0:T(8,128)S(1)} collective-permute-done((f32[8,128]{1,0:T(8,128)}, f32[8,128]{1,0:T(8,128)S(1)}, u32[]{:S(2)}, u32[]{:S(2)}) %collective-permute-start) | collective-permute-done | bytes 4128 | tf_op jit(solution)/shard_map/ppermute | solution.py:203
  27.6 1.4 %broadcast_add_fusion = f32[8,8,128]{2,1,0:T(8,128)} fusion(f32[8,8,128]{2,1,0:T(8,128)} %get-tuple-element.15, f32[8,128]{1,0:T(8,128)S(1)} %collective-permute-done), kind=kLoop, calls=%fused_computation | loop fusion | flops 8192 | bytes 69632 | tf_op jit(solution)/shard_map/add | solution.py:205
  29.0 2.5 %all-to-all-done.surface = f32[8,8,1152]{2,1,0:T(8,128)S(1)} async-done(((f32[8,8,1152]{2,1,0:T(8,128)}), f32[8,8,1152]{2,1,0:T(8,128)S(1)}, u32[]{:S(2)}, u32[]{:S(2)}) %all-to-all-start) | async-done | bytes 294944 | tf_op jit(solution)/shard_map/all_to_all | solution.py:204
  31.4 7.6 %all-to-all-start.1 = ((f32[8,8,128]{2,1,0:T(8,128)}), f32[8,8,128]{2,1,0:T(8,128)S(1)}, u32[]{:S(2)}, u32[]{:S(2)}) async-start(f32[8,8,128]{2,1,0:T(8,128)} %broadcast_add_fusion), calls=%async_computation.1 | async-start | bytes 65536 | tf_op jit(solution)/shard_map/all_to_all | solution.py:206
  39.0 0.0 copy-start.1
  39.0 0.7 copy-done.1
  39.7 2.1 %shard_map.78 = (bf16[8192,128]{1,0:T(8,128)(2,1)S(1)}, bf16[16,8192]{1,0:T(8,128)(2,1)S(1)}, f32[8,128]{1,0:T(8,128)S(1)}) custom-call(f32[3,128]{1,0:T(4,128)S(1)} %copy-done.1, f32[8,8,1152]{2,1,0:T(8,128)S(1)} %all-to-all-done.surface), custom_call_target="tpu_custom_call" | custom-call | flops 5000000000 | bytes 3145728 | tf_op jit(solution)/shard_map/pallas_call | solution.py:208
  41.8 5.2 %all-to-all-done.1.nodes = f32[8,8,128]{2,1,0:T(8,128)S(1)} async-done(((f32[8,8,128]{2,1,0:T(8,128)}), f32[8,8,128]{2,1,0:T(8,128)S(1)}, u32[]{:S(2)}, u32[]{:S(2)}) %all-to-all-start.1) | async-done | bytes 32800 | tf_op jit(solution)/shard_map/all_to_all | solution.py:206
  47.0 0.0 copy-start
  47.0 10.3 %shard_map.79 = (f32[8,8,256]{2,1,0:T(8,128)S(1)}, f32[8,256]{1,0:T(8,128)S(1)}) custom-call(s32[1]{0:T(128)} %bitcast.place, f32[8,8,128]{2,1,0:T(8,128)S(1)} %all-to-all-done.1.nodes, bf16[8192,128]{1,0:T(8,128)(2,1)S(1)} %get-tuple-element.19.right, bf16[16,8192]{1,0:T(8,128)(2,1)S(1)} %get-tuple-element.20.terms, f32[8,128]{1,0:T(8,128)S(1)} %get-tuple-element.21.own_sums), custom_call_target="tpu_custom_call" | custom-call | flops 30000001024 | bytes 3145728 | tf_op jit(solution)/shard_map/pallas_call | solution.py:221
  57.3 10.8 %all_to_all.15.received = f32[8,8,256]{2,1,0:T(8,128)S(1)} all-to-all(f32[8,8,256]{2,1,0:T(8,128)S(1)} %get-tuple-element.22), channel_id=1, replica_groups=mesh['vol'=16,'z'=8,'y'=8] {'y'}, dimensions={0} | all-to-all | bytes 131072 | tf_op jit(solution)/shard_map/all_to_all | solution.py:238
  68.1 0.0 copy-done
  68.1 0.8 %shard_map.80 = (f32[3,128]{1,0:T(4,128)}, f32[4,128]{1,0:T(4,128)}) custom-call(f32[8,8,256]{2,1,0:T(8,128)S(1)} %all_to_all.15.received, f32[8,256]{1,0:T(8,128)S(1)} %get-tuple-element.23.near, s32[4,512]{1,0:T(4,128)S(1)} %copy-done), custom_call_target="tpu_custom_call" | custom-call | tf_op jit(solution)/shard_map/pallas_call | solution.py:240
Async XLA Ops:
  2.2 29.3 %all-to-all-start = ((f32[8,8,1152]{2,1,0:T(8,128)}), f32[8,8,1152]{2,1,0:T(8,128)S(1)}, u32[]{:S(2)}, u32[]{:S(2)}) async-start(f32[8,8,1152]{2,1,0:T(8,128)} %get-tuple-element.14), calls=%async_computation | async-start | bytes 589824 | tf_op jit(solution)/shard_map/all_to_all | solution.py:204
  18.8 8.8 %collective-permute-start = (f32[8,128]{1,0:T(8,128)}, f32[8,128]{1,0:T(8,128)S(1)}, u32[]{:S(2)}, u32[]{:S(2)}) collective-permute-start(f32[8,128]{1,0:T(8,128)} %get-tuple-element.16), channel_id=1, source_target_pairs={{7,15},{8,0},{15,23},{16,8},{23,31},{24,16},{31,39},{32,24},{39,47... | collective-permute-start | bytes 12296 | tf_op jit(solution)/shard_map/ppermute | solution.py:203
  31.4 15.6 %all-to-all-start.1 = ((f32[8,8,128]{2,1,0:T(8,128)}), f32[8,8,128]{2,1,0:T(8,128)S(1)}, u32[]{:S(2)}, u32[]{:S(2)}) async-start(f32[8,8,128]{2,1,0:T(8,128)} %broadcast_add_fusion), calls=%async_computation.1 | async-start | bytes 65536 | tf_op jit(solution)/shard_map/all_to_all | solution.py:206
  39.0 0.7 copy-start.1
  47.0 21.1 %copy-start = (s32[4,512]{1,0:T(4,128)S(1)}, s32[4,512]{1,0:T(4,128)}, u32[]{:S(2)}) copy-start(s32[4,512]{1,0:T(4,128)} %cells.1) | copy-start | bytes 24580

commit v5 on v4

--- a/solution.py
+++ b/solution.py
@@ -83,7 +83,7 @@
     return jnp.concatenate(stack, axis=0).T.astype(BF16)
 
 
-def add_sums(right, terms, left, total, surf_step):
+def add_sums(right, terms, left, total, surf_step, first=0):
     def step(i, carry):
         s = pl.multiple_of(i * surf_step, LANES)
         spread = jnp.dot(right[pl.ds(s, surf_step), :], left[...], preferred_element_type=F32)
@@ -97,14 +97,13 @@
         )
         return carry
 
-    total[...] = jnp.zeros_like(total)
-    lax.fori_loop(0, right.shape[0] // surf_step, step, 0)
-
-
-def own_kernel(points, surface, right, terms, sums, left, total):
+    lax.fori_loop(first // surf_step, right.shape[0] // surf_step, step, 0)
+
+
+def surface_operands(surface, right, terms):
     width = surface.shape[2] - LANES
     line = rows_of((SIDE, width))
-    for part in range(SIDE):
+    for part in range(surface.shape[0]):
         value = surface[part][:, :width]
         tail = surface[part][:, width:]
         tail = jnp.concatenate([tail[i : i + 1] for i in range(SIDE)], axis=1)
@@ -112,21 +111,46 @@
         term = jnp.where(line < 5, value, jnp.where(line == 5, tail, jnp.where(line == 6, 1.0, 0.0)))
         high, middle, _ = in_three(term)
         terms[:, part * width : (part + 1) * width] = jnp.concatenate([high, middle], axis=0).astype(BF16)
-    left[...] = node_side(jnp.concatenate([jnp.zeros((5, LANES), F32), points[...]], axis=0))
-    add_sums(right, terms, left, total, OWN_STEP)
-    sums[...] = total[:SIDE] + total[SIDE:]
-
-
-def sums_kernel(place, nodes, right, terms, own_sums, message, near, left, total, sums, spots):
+
+
+def early_kernel(nodes, surface, result, right, terms, left, total):
+    surface_operands(surface, right, terms)
+    for block in range(SIDE):
+        left[:, block * LANES : (block + 1) * LANES] = node_side(nodes[block])
+    total[...] = jnp.zeros_like(total)
+    add_sums(right, terms, left, total, SURF_STEP)
+    for block in range(SIDE):
+        result[block, :SIDE] = nodes[block]
+        result[block, SIDE:] = total[:, block * LANES : (block + 1) * LANES]
+
+
+def own_kernel(flag, points, surface, before, right, terms, sums, left, total):
+    surface_operands(surface, right, terms)
+
+    @pl.when(flag[0] == 1)
+    def _():
+        for block in range(SIDE):
+            left[:, block * LANES : (block + 1) * LANES] = node_side(before[block, :SIDE])
+            total[:, block * LANES : (block + 1) * LANES] = before[block, SIDE:]
+        add_sums(right, terms, left, total, SURF_STEP, right.shape[0] // 2)
+        sums[...] = total[:SIDE] + total[SIDE:]
+
+    @pl.when(flag[0] == 0)
+    def _():
+        left[:, :LANES] = node_side(jnp.concatenate([jnp.zeros((5, LANES), F32), points[...]], axis=0))
+        total[:, :LANES] = jnp.zeros((16, LANES), F32)
+        add_sums(right, terms, left.at[:, :LANES], total.at[:, :LANES], OWN_STEP)
+        sums[:, :LANES] = total[:SIDE, :LANES] + total[SIDE:, :LANES]
+
+
+def sums_kernel(place, nodes, right, terms, known, message, near, left, total, sums, spots):
     lane = lanes_of((SIDE, LANES))
-    here = place[0]
+    here, early = place[0], place[1]
     outer = jnp.where(lane < 32, nodes[SIDE - 1], pltpu.roll(nodes[0], 32, axis=1))
     outer = pltpu.roll(outer, 5, axis=0)
-    for k in range(SIDE):
-        value = nodes[(here + k + 1) % SIDE] if k < SIDE - 1 else outer
-        left[:, k * LANES : (k + 1) * LANES] = node_side(value)
-    add_sums(right, terms, left, total, SURF_STEP)
-    whole = total[:SIDE] + total[SIDE:]
+    end = (SIDE - 1) * LANES
+    left[:, end:] = node_side(outer)
+    total[...] = jnp.zeros_like(total)
 
     def keep(block, value):
         message[block, :, :LANES] = value
@@ -134,10 +158,23 @@
         sums[block + 1] = pick_lanes(value, index)
         spots[block + 1] = pick_lanes(nodes[block], index)
 
-    keep(here, own_sums[...])
-    for k in range(SIDE - 1):
-        keep((here + k + 1) % SIDE, whole[:, k * LANES : (k + 1) * LANES])
-    value = whole[:, (SIDE - 1) * LANES :]
+    @pl.when(early == 1)
+    def _():
+        add_sums(right, terms, left.at[:, end:], total.at[:, end:], OWN_STEP)
+        for block in range(SIDE):
+            keep(block, known[:, block * LANES : (block + 1) * LANES])
+
+    @pl.when(early == 0)
+    def _():
+        for k in range(SIDE - 1):
+            left[:, k * LANES : (k + 1) * LANES] = node_side(nodes[(here + k + 1) % SIDE])
+        add_sums(right, terms, left, total, SURF_STEP)
+        keep(here, known[:, :LANES])
+        for k in range(SIDE - 1):
+            part = total[:, k * LANES : (k + 1) * LANES]
+            keep((here + k + 1) % SIDE, part[:SIDE] + part[SIDE:])
+
+    value = total[:SIDE, end:] + total[SIDE:, end:]
     sums[0] = value
     sums[SIDE + 1] = pltpu.roll(value, LANES - 32, axis=1)
     spots[0] = outer
@@ -195,36 +232,60 @@
         ),
         scratch_shapes=[pltpu.VMEM((8, LANES), jnp.int32)],
     )(points, surface, displacement, rotation, halo_index.reshape(1, lend))
+    total_surface = SIDE * width
+    early = lax.axis_index("zh") == 0
+
+    def ahead():
+        beside = lax.all_to_all(own, "y", 0, 0)
+        near_surfaces = lax.all_to_all(message[: SIDE // 2], "zl", 0, 0)
+        return pl.pallas_call(
+            early_kernel,
+            out_shape=jax.ShapeDtypeStruct((SIDE, 24, nodes), F32),
+            scratch_shapes=[
+                pltpu.VMEM((total_surface // 2, LANES), BF16),
+                pltpu.VMEM((16, total_surface // 2), BF16),
+                pltpu.VMEM((LANES, SIDE * LANES), BF16),
+                pltpu.VMEM((16, SIDE * LANES), F32),
+            ],
+            compiler_params=pltpu.CompilerParams(vmem_limit_bytes=40 << 20),
+            cost_estimate=pl.CostEstimate(flops=15 * 10**9, bytes_accessed=1 << 20, transcendentals=4 << 20),
+        )(beside, near_surfaces)
+
+    before = lax.cond(early, ahead, lambda: jnp.zeros((SIDE, 24, nodes), F32))
+    message, lent, before = lax.optimization_barrier((message, lent, before))
     rows = lax.axis_size("vol") * SIDE
     ends = []
     for row in range(rows):
         after = (row + 1) % rows
         ends += [(row * SIDE + SIDE - 1, after * SIDE + SIDE - 1), (after * SIDE, row * SIDE)]
-    outer = lax.ppermute(lent, ("vol", "z", "y"), ends)
-    surfaces = lax.all_to_all(message, "z", 0, 0)
+    outer = lax.ppermute(lent, ("vol", "zh", "zl", "y"), ends)
+    surfaces = lax.all_to_all(message, ("zh", "zl"), 0, 0)
     surfaces, ready = lax.optimization_barrier((surfaces, own + outer))
     around = lax.all_to_all(ready, "y", 0, 0)
-    total_surface = SIDE * width
-    right, terms, own_sums = pl.pallas_call(
+    flag = early.astype(jnp.int32)
+    vmem = pl.BlockSpec(memory_space=pltpu.VMEM)
+    smem = pl.BlockSpec(memory_space=pltpu.SMEM)
+    right, terms, known = pl.pallas_call(
         own_kernel,
         out_shape=(
             jax.ShapeDtypeStruct((total_surface, LANES), BF16),
             jax.ShapeDtypeStruct((16, total_surface), BF16),
-            jax.ShapeDtypeStruct((8, LANES), F32),
+            jax.ShapeDtypeStruct((8, SIDE * LANES), F32),
         ),
-        scratch_shapes=[pltpu.VMEM((LANES, LANES), BF16), pltpu.VMEM((16, LANES), F32)],
-        compiler_params=pltpu.CompilerParams(vmem_limit_bytes=24 << 20),
-        cost_estimate=pl.CostEstimate(flops=5 * 10**9, bytes_accessed=3 << 20, transcendentals=1 << 20),
-    )(points, surfaces)
-    place = lax.axis_index("y").astype(jnp.int32).reshape(1)
-    vmem = pl.BlockSpec(memory_space=pltpu.VMEM)
+        in_specs=[smem, vmem, vmem, vmem],
+        out_specs=(vmem, vmem, vmem),
+        scratch_shapes=[pltpu.VMEM((LANES, SIDE * LANES), BF16), pltpu.VMEM((16, SIDE * LANES), F32)],
+        compiler_params=pltpu.CompilerParams(vmem_limit_bytes=40 << 20),
+        cost_estimate=pl.CostEstimate(flops=15 * 10**9, bytes_accessed=3 << 20, transcendentals=4 << 20),
+    )(flag.reshape(1), points, surfaces, before)
+    place = jnp.stack([lax.axis_index("y").astype(jnp.int32), flag])
     partial, near = pl.pallas_call(
         sums_kernel,
         out_shape=(
             jax.ShapeDtypeStruct((SIDE, 8, 2 * LANES), F32),
             jax.ShapeDtypeStruct((8, 2 * LANES), F32),
         ),
-        in_specs=[pl.BlockSpec(memory_space=pltpu.SMEM), vmem, vmem, vmem, vmem],
+        in_specs=[smem, vmem, vmem, vmem, vmem],
         out_specs=(vmem, vmem),
         scratch_shapes=[
             pltpu.VMEM((LANES, SIDE * LANES), BF16),
@@ -234,7 +295,7 @@
         ],
         compiler_params=pltpu.CompilerParams(vmem_limit_bytes=40 << 20),
         cost_estimate=pl.CostEstimate(flops=30 * 10**9, bytes_accessed=3 << 20, transcendentals=8 << 20),
-    )(place, around, right, terms, own_sums)
+    )(place, around, right, terms, known)
     received = lax.all_to_all(partial, "y", 0, 0)
     count = connectivity.shape[1]
     motion, swept = pl.pallas_call(
@@ -249,9 +310,9 @@
 
 
 def solution(mesh):
-    split = Mesh(mesh.devices.reshape(mesh.devices.shape[0], SIDE, SIDE), ("vol", "z", "y"))
-    nodes = ("vol", "z", "y")
-    surface = P(None, ("z", "y"))
+    split = Mesh(mesh.devices.reshape(mesh.devices.shape[0], 2, SIDE // 2, SIDE), ("vol", "zh", "zl", "y"))
+    nodes = ("vol", "zh", "zl", "y")
+    surface = P(None, ("zh", "zl", "y"))
     in_specs = (P(None, nodes), surface, surface, surface, P(nodes), P(None, nodes))
     out_specs = (P(None, nodes), P(nodes))
     return jax.shard_map(shards, mesh=split, in_specs=in_specs, out_specs=out_specs, check_vma=False)

time: 69.4 us -> 82.2 us (1.18)
  blocking collectives: 10.8 us -> 29.6 us
  starting transfers between devices: 29.1 us -> 16.8 us
  waiting for transfers between devices: 11.5 us -> 16.7 us
  Pallas kernels: 14.7 us -> 16.2 us
    all_to_all x0 -> x1, blocking collectives: none -> 16.4 us  [ahead(): near_surfaces = lax.all_to_all(message[:SIDE // 2], 'zl', 0, 0)]
    all_to_all x1 -> x2, waiting for transfers between devices: 2.45 us -> 11 us  [the longest x1 6.89 us: ahead(): beside = lax.all_to_all(own, 'y', 0, 0)]
    pallas_call x1, Pallas kernels: 10.3 us -> 2.67 us  [shards(): pl.pallas_call(sums_kernel, out_shape=(jax.ShapeDtypeStruct((SIDE, 8, 2 *...]
    all_to_all x1 -> x2, starting transfers between devices: 16.7 us -> 11.1 us  [the longest x1 7.69 us: ahead(): beside = lax.all_to_all(own, 'y', 0, 0)]
    pallas_call x0 -> x1, Pallas kernels: none -> 5.46 us  [ahead(): pl.pallas_call(early_kernel, out_shape=jax.ShapeDtypeStruct((SIDE, 24, no...]
    all_to_all x1, starting transfers between devices: 7.56 us -> 3.34 us  [shards(): around = lax.all_to_all(ready, 'y', 0, 0)]
    pallas_call x1, Pallas kernels: 2.12 us -> 5.81 us  [shards(): pl.pallas_call(own_kernel, out_shape=(jax.ShapeDtypeStruct((total_surface...]
    all_to_all x1, waiting for transfers between devices: 5.22 us -> 2.12 us  [shards(): around = lax.all_to_all(ready, 'y', 0, 0)]
  transfers between devices with their start and end apart: 3 -> 4, of which waited for: 3 -> 4; matrix products, arithmetic and copies ran while one was open for 2% -> 2% of each run, Pallas kernels for 3% -> 7%
where the time goes in v5:
time: 82.2 us; the launch traced here: 81.7 us
  blocking collectives  29.6 us (36%)
  starting transfers between devices  16.8 us (20%)
  waiting for transfers between devices  16.7 us (20%)
  Pallas kernels  16.2 us (20%)
  local copies, waits for them, and re-layouts  0.93 us (1%)
    all_to_all x1, blocking collectives, ahead(): near_surfaces = lax.all_to_all(message[:SIDE // 2], 'zl', 0, 0)  16.4 us
    all_to_all x1, blocking collectives, shards(): received = lax.all_to_all(partial, 'y', 0, 0)  13.2 us
    all_to_all x1, starting transfers between devices, ahead(): beside = lax.all_to_all(own, 'y', 0, 0)  7.69 us
    all_to_all x1, waiting for transfers between devices, ahead(): beside = lax.all_to_all(own, 'y', 0, 0)  6.89 us
    pallas_call x1, Pallas kernels, shards(): pl.pallas_call(own_kernel, out_shape=(jax.ShapeDtypeStruct((total_surface...  5.81 us
    pallas_call x1, Pallas kernels, ahead(): pl.pallas_call(early_kernel, out_shape=jax.ShapeDtypeStruct((SIDE, 24, no...  5.46 us
    all_to_all x1, waiting for transfers between devices, shards(): surfaces = lax.all_to_all(message, ('zh', 'zl'), 0, 0)  4.11 us
    ppermute x1, waiting for transfers between devices, shards(): outer = lax.ppermute(lent, ('vol', 'zh', 'zl', 'y'), ends)  3.59 us
  transfers between devices with their start and end apart: 4, of which 4 were waited for; matrix products, arithmetic and copies ran while one was open for 2% of the time, Pallas kernels for 7%

profile of v5, /device:TPU:14, one launch (start us, length us, event | category | flops | bytes accessed | tf_op | source)
XLA Modules:
  0.0 81.7 jit_solution(15863266210040831532)
XLA Ops:
  0.6 1.5 %shard_map.77 = (f32[8,8,1152]{2,1,0:T(8,128)}, f32[8,8,128]{2,1,0:T(8,128)S(1)}, f32[8,128]{1,0:T(8,128)}) custom-call(f32[3,128]{1,0:T(4,128)} %points.3, f32[3,1024]{1,0:T(4,128)} %surface.1, f32[3,1024]{1,0:T(4,128)} %displacement.1, f32[3,1024]{1,0:T(4,128)} %rotation.1, s32[1,32]{1,0:T(1,128)} %bitcast.4), custom_call_target="tpu_custom_call" | custom-call | tf_op jit(solution)/shard_map/pallas_call | solution.py:226
  2.2 0.0 copy-start.2
  2.2 0.0 copy-start.1
  2.2 37.4 %conditional.1 = (f32[8,24,128]{2,1,0:T(8,128)S(1)}) conditional(s32[]{:T(128)} %convert_element_type.4, () %tuple.16, (f32[8,8,128]{2,1,0:T(8,128)S(1)}, f32[8,8,1152]{2,1,0:T(8,128)}) %tuple.17), branch_computations={%region_0.0_spmd, %region_1.0_spmd} | conditional | flops 15000000512 | bytes 1736744 | solution.py:254
  2.2 7.7 %all-to-all-start = ((f32[8,8,128]{2,1,0:T(8,128)S(1)}), f32[8,8,128]{2,1,0:T(8,128)S(1)}, u32[]{:S(2)}, u32[]{:S(2)}) async-start(f32[8,8,128]{2,1,0:T(8,128)S(1)} %get-tuple-element.4), calls=%async_computation | async-start | bytes 65536 | tf_op jit(solution)/shard_map/cond/branch_1_fun/all_to_all | solution.py:239
  9.9 0.9 %slice.2 = f32[4,8,1152]{2,1,0:T(8,128)S(1)} slice(f32[8,8,1152]{2,1,0:T(8,128)} %get-tuple-element.8), slice={[0:4], [0:8], [0:1152]} | slice | bytes 294912 | tf_op jit(solution)/shard_map/cond/branch_1_fun/slice | solution.py:240
  10.8 6.9 %all-to-all-done.nodes = f32[8,8,128]{2,1,0:T(8,128)S(1)} async-done(((f32[8,8,128]{2,1,0:T(8,128)S(1)}), f32[8,8,128]{2,1,0:T(8,128)S(1)}, u32[]{:S(2)}, u32[]{:S(2)}) %all-to-all-start) | async-done | bytes 32800 | tf_op jit(solution)/shard_map/cond/branch_1_fun/all_to_all | solution.py:239
  17.7 16.4 %all_to_all.23.surface = f32[4,8,1152]{2,1,0:T(8,128)S(1)} all-to-all(f32[4,8,1152]{2,1,0:T(8,128)S(1)} %slice.2), channel_id=1, replica_groups=mesh['vol'=16,'zh'=2,'zl'=4,'y'=8] {'zl'}, dimensions={0} | all-to-all | bytes 294912 | tf_op jit(solution)/shard_map/cond/branch_1_fun/all_to_all | solution.py:240
  34.1 5.5 %branch_1_fun.1 = f32[8,24,128]{2,1,0:T(8,128)S(1)} custom-call(f32[8,8,128]{2,1,0:T(8,128)S(1)} %all-to-all-done.nodes, f32[4,8,1152]{2,1,0:T(8,128)S(1)} %all_to_all.23.surface), custom_call_target="tpu_custom_call" | custom-call | flops 15000000512 | bytes 1048576 | tf_op jit(solution)/shard_map/cond/branch_1_fun/pallas_call | solution.py:241
  39.6 3.4 %all-to-all-start.2 = ((f32[8,8,1152]{2,1,0:T(8,128)}), f32[8,8,1152]{2,1,0:T(8,128)S(1)}, u32[]{:S(2)}, u32[]{:S(2)}) async-start(f32[8,8,1152]{2,1,0:T(8,128)} %get-tuple-element.29), calls=%async_computation.2 | async-start | bytes 589824 | tf_op jit(solution)/shard_map/all_to_all | solution.py:262
  43.0 0.0 copy-done.2
  43.0 2.3 %collective-permute-start = (f32[8,128]{1,0:T(8,128)S(1)}, f32[8,128]{1,0:T(8,128)S(1)}, u32[]{:S(2)}, u32[]{:S(2)}) collective-permute-start(f32[8,128]{1,0:T(8,128)S(1)} %copy-done.2), channel_id=1, source_target_pairs={{7,15},{8,0},{15,23},{16,8},{23,31},{24,16},{31,39},{32,24},{39,47... | collective-permute-start | bytes 12296 | tf_op jit(solution)/shard_map/ppermute | solution.py:261
  45.4 0.1 pad_add_fusion.place
  45.4 3.6 %collective-permute-done = f32[8,128]{1,0:T(8,128)S(1)} collective-permute-done((f32[8,128]{1,0:T(8,128)S(1)}, f32[8,128]{1,0:T(8,128)S(1)}, u32[]{:S(2)}, u32[]{:S(2)}) %collective-permute-start) | collective-permute-done | bytes 4128 | tf_op jit(solution)/shard_map/ppermute | solution.py:261
  49.0 0.6 broadcast_add_fusion
  49.6 4.1 %all-to-all-done.2.surface = f32[8,8,1152]{2,1,0:T(8,128)S(1)} async-done(((f32[8,8,1152]{2,1,0:T(8,128)}), f32[8,8,1152]{2,1,0:T(8,128)S(1)}, u32[]{:S(2)}, u32[]{:S(2)}) %all-to-all-start.2) | async-done | bytes 294944 | tf_op jit(solution)/shard_map/all_to_all | solution.py:262
  53.8 3.3 %all-to-all-start.3 = ((f32[8,8,128]{2,1,0:T(8,128)}), f32[8,8,128]{2,1,0:T(8,128)S(1)}, u32[]{:S(2)}, u32[]{:S(2)}) async-start(f32[8,8,128]{2,1,0:T(8,128)} %broadcast_add_fusion), calls=%async_computation.3 | async-start | bytes 65536 | tf_op jit(solution)/shard_map/all_to_all | solution.py:264
  57.1 0.0 copy-done.1
  57.1 5.8 %shard_map.78 = (bf16[8192,128]{1,0:T(8,128)(2,1)S(1)}, bf16[16,8192]{1,0:T(8,128)(2,1)S(1)}, f32[8,1024]{1,0:T(8,128)S(1)}) custom-call(s32[1]{0:T(128)} %bitcast.1.flag, f32[3,128]{1,0:T(4,128)S(1)} %copy-done.1, f32[8,8,1152]{2,1,0:T(8,128)S(1)} %all-to-all-done.2.surface, f32[8,24,128]{2,1,0:T(8,128)S(1)} %get-tuple-element.41.before), custom_call_target="tpu_custom_call" | custom-call | flops 15000000512 | bytes 3145728 | tf_op jit(solution)/shard_map/pallas_call | solution.py:268
  62.9 2.1 %all-to-all-done.3.nodes = f32[8,8,128]{2,1,0:T(8,128)S(1)} async-done(((f32[8,8,128]{2,1,0:T(8,128)}), f32[8,8,128]{2,1,0:T(8,128)S(1)}, u32[]{:S(2)}, u32[]{:S(2)}) %all-to-all-start.3) | async-done | bytes 32800 | tf_op jit(solution)/shard_map/all_to_all | solution.py:264
  65.0 2.7 %shard_map.79 = (f32[8,8,256]{2,1,0:T(8,128)S(1)}, f32[8,256]{1,0:T(8,128)S(1)}) custom-call(s32[2]{0:T(128)S(1)} %pad_add_fusion.place, f32[8,8,128]{2,1,0:T(8,128)S(1)} %all-to-all-done.3.nodes, bf16[8192,128]{1,0:T(8,128)(2,1)S(1)} %get-tuple-element.34.right, bf16[16,8192]{1,0:T(8,128)(2,1)S(1)} %get-tuple-element.35.terms, ...), custom_call_target="tpu_custom_call" | custom-call | flops 30000001024 | bytes 3145728 | tf_op jit(solution)/shard_map/pallas_call | solution.py:282
  67.7 13.2 %all_to_all.24.received = f32[8,8,256]{2,1,0:T(8,128)S(1)} all-to-all(f32[8,8,256]{2,1,0:T(8,128)S(1)} %get-tuple-element.37), channel_id=1, replica_groups=mesh['vol'=16,'zh'=2,'zl'=4,'y'=8] {'y'}, dimensions={0} | all-to-all | bytes 131072 | tf_op jit(solution)/shard_map/all_to_all | solution.py:299
  80.9 0.0 copy-done
  80.9 0.8 shard_map.80
  (1 shorter events, 0.0 us)
Async XLA Ops:
  2.2 40.9 %copy-start.2 = (f32[8,128]{1,0:T(8,128)S(1)}, f32[8,128]{1,0:T(8,128)}, u32[]{:S(2)}) copy-start(f32[8,128]{1,0:T(8,128)} %get-tuple-element.30) | copy-start | bytes 12292
  2.2 54.9 %copy-start.1 = (f32[3,128]{1,0:T(4,128)S(1)}, f32[3,128]{1,0:T(4,128)}, u32[]{:S(2)}) copy-start(f32[3,128]{1,0:T(4,128)} %points.3) | copy-start | bytes 4612
  2.2 15.5 %all-to-all-start = ((f32[8,8,128]{2,1,0:T(8,128)S(1)}), f32[8,8,128]{2,1,0:T(8,128)S(1)}, u32[]{:S(2)}, u32[]{:S(2)}) async-start(f32[8,8,128]{2,1,0:T(8,128)S(1)} %get-tuple-element.4), calls=%async_computation | async-start | bytes 65536 | tf_op jit(solution)/shard_map/cond/branch_1_fun/all_to_all | solution.py:239
  39.6 14.2 %all-to-all-start.2 = ((f32[8,8,1152]{2,1,0:T(8,128)}), f32[8,8,1152]{2,1,0:T(8,128)S(1)}, u32[]{:S(2)}, u32[]{:S(2)}) async-start(f32[8,8,1152]{2,1,0:T(8,128)} %get-tuple-element.29), calls=%async_computation.2 | async-start | bytes 589824 | tf_op jit(solution)/shard_map/all_to_all | solution.py:262
  43.0 6.0 %collective-permute-start = (f32[8,128]{1,0:T(8,128)S(1)}, f32[8,128]{1,0:T(8,128)S(1)}, u32[]{:S(2)}, u32[]{:S(2)}) collective-permute-start(f32[8,128]{1,0:T(8,128)S(1)} %copy-done.2), channel_id=1, source_target_pairs={{7,15},{8,0},{15,23},{16,8},{23,31},{24,16},{31,39},{32,24},{39,47... | collective-permute-start | bytes 12296 | tf_op jit(solution)/shard_map/ppermute | solution.py:261
  53.8 11.3 %all-to-all-start.3 = ((f32[8,8,128]{2,1,0:T(8,128)}), f32[8,8,128]{2,1,0:T(8,128)S(1)}, u32[]{:S(2)}, u32[]{:S(2)}) async-start(f32[8,8,128]{2,1,0:T(8,128)} %broadcast_add_fusion), calls=%async_computation.3 | async-start | bytes 65536 | tf_op jit(solution)/shard_map/all_to_all | solution.py:264
  65.0 15.9 %copy-start = (s32[4,512]{1,0:T(4,128)S(1)}, s32[4,512]{1,0:T(4,128)}, u32[]{:S(2)}) copy-start(s32[4,512]{1,0:T(4,128)} %cells.1) | copy-start | bytes 24580

commit v6 on v4

--- a/solution.py
+++ b/solution.py
@@ -120,7 +120,7 @@
 def sums_kernel(place, nodes, right, terms, own_sums, message, near, left, total, sums, spots):
     lane = lanes_of((SIDE, LANES))
     here = place[0]
-    outer = jnp.where(lane < 32, nodes[SIDE - 1], pltpu.roll(nodes[0], 32, axis=1))
+    outer = jnp.where(lane < 32, nodes[0], pltpu.roll(nodes[1], 32, axis=1))
     outer = pltpu.roll(outer, 5, axis=0)
     for k in range(SIDE):
         value = nodes[(here + k + 1) % SIDE] if k < SIDE - 1 else outer
@@ -194,12 +194,13 @@
             jax.ShapeDtypeStruct((8, LANES), F32),
         ),
         scratch_shapes=[pltpu.VMEM((8, LANES), jnp.int32)],
+        cost_estimate=pl.CostEstimate(flops=3 * 10**9, bytes_accessed=8 << 20, transcendentals=0),
     )(points, surface, displacement, rotation, halo_index.reshape(1, lend))
     rows = lax.axis_size("vol") * SIDE
     ends = []
     for row in range(rows):
         after = (row + 1) % rows
-        ends += [(row * SIDE + SIDE - 1, after * SIDE + SIDE - 1), (after * SIDE, row * SIDE)]
+        ends += [(row * SIDE + SIDE - 1, after * SIDE), (after * SIDE, row * SIDE + 1)]
     outer = lax.ppermute(lent, ("vol", "z", "y"), ends)
     surfaces = lax.all_to_all(message, "z", 0, 0)
     surfaces, ready = lax.optimization_barrier((surfaces, own + outer))

time: 69.4 us -> 69.4 us (level)
  starting transfers between devices: 29.1 us -> 30.2 us
    ppermute x1, starting transfers between devices: 4.88 us -> 6.01 us  [shards(): outer = lax.ppermute(lent, ('vol', 'z', 'y'), ends)]
where the time goes in v6:
time: 69.4 us; the launch traced here: 69 us
  starting transfers between devices  30.2 us (44%)
  Pallas kernels  14.8 us (21%)
  waiting for transfers between devices  11.2 us (16%)
  blocking collectives  10.8 us (16%)
  other arithmetic  1.37 us (2%)
    all_to_all x1, starting transfers between devices, shards(): surfaces = lax.all_to_all(message, 'z', 0, 0)  16.7 us
    all_to_all x1, blocking collectives, shards(): received = lax.all_to_all(partial, 'y', 0, 0)  10.8 us
    pallas_call x1, Pallas kernels, shards(): pl.pallas_call(sums_kernel, out_shape=(jax.ShapeDtypeStruct((SIDE, 8, 2 *...  10.4 us
    all_to_all x1, starting transfers between devices, shards(): around = lax.all_to_all(ready, 'y', 0, 0)  7.48 us
    ppermute x1, starting transfers between devices, shards(): outer = lax.ppermute(lent, ('vol', 'z', 'y'), ends)  6.01 us
    all_to_all x1, waiting for transfers between devices, shards(): around = lax.all_to_all(ready, 'y', 0, 0)  5.9 us
    ppermute x1, waiting for transfers between devices, shards(): outer = lax.ppermute(lent, ('vol', 'z', 'y'), ends)  3.43 us
    pallas_call x1, Pallas kernels, shards(): pl.pallas_call(own_kernel, out_shape=(jax.ShapeDtypeStruct((total_surface...  2.12 us
  transfers between devices with their start and end apart: 3, of which 3 were waited for; matrix products, arithmetic and copies ran while one was open for 2% of the time, Pallas kernels for 3%

profile of v6, /device:TPU:14, one launch (start us, length us, event | category | flops | bytes accessed | tf_op | source)
XLA Modules:
  0.0 69.0 jit_solution(1626929769359994219)
XLA Ops:
  0.6 0.0 copy-start.1
  0.6 1.5 %shard_map.77 = (f32[8,8,1152]{2,1,0:T(8,128)}, f32[8,8,128]{2,1,0:T(8,128)}, f32[8,128]{1,0:T(8,128)}) custom-call(f32[3,128]{1,0:T(4,128)} %points.3, f32[3,1024]{1,0:T(4,128)} %surface.1, f32[3,1024]{1,0:T(4,128)} %displacement.1, f32[3,1024]{1,0:T(4,128)} %rotation.1, s32[1,32]{1,0:T(1,128)} %bitcast.4), custom_call_target="tpu_custom_call" | custom-call | flops 3000000000 | bytes 8388608 | tf_op jit(solution)/shard_map/pallas_call | solution.py:189
  2.2 16.7 %all-to-all-start = ((f32[8,8,1152]{2,1,0:T(8,128)}), f32[8,8,1152]{2,1,0:T(8,128)S(1)}, u32[]{:S(2)}, u32[]{:S(2)}) async-start(f32[8,8,1152]{2,1,0:T(8,128)} %get-tuple-element.14), calls=%async_computation | async-start | bytes 589824 | tf_op jit(solution)/shard_map/all_to_all | solution.py:205
  18.9 6.0 %collective-permute-start = (f32[8,128]{1,0:T(8,128)}, f32[8,128]{1,0:T(8,128)S(1)}, u32[]{:S(2)}, u32[]{:S(2)}) collective-permute-start(f32[8,128]{1,0:T(8,128)} %get-tuple-element.16), channel_id=1, source_target_pairs={{7,8},{8,1},{15,16},{16,9},{23,24},{24,17},{31,32},{32,25},{39,40}... | collective-permute-start | bytes 12296 | tf_op jit(solution)/shard_map/ppermute | solution.py:204
  24.9 3.4 %collective-permute-done = f32[8,128]{1,0:T(8,128)S(1)} collective-permute-done((f32[8,128]{1,0:T(8,128)}, f32[8,128]{1,0:T(8,128)S(1)}, u32[]{:S(2)}, u32[]{:S(2)}) %collective-permute-start) | collective-permute-done | bytes 4128 | tf_op jit(solution)/shard_map/ppermute | solution.py:204
  28.3 1.4 %broadcast_add_fusion = f32[8,8,128]{2,1,0:T(8,128)} fusion(f32[8,8,128]{2,1,0:T(8,128)} %get-tuple-element.15, f32[8,128]{1,0:T(8,128)S(1)} %collective-permute-done), kind=kLoop, calls=%fused_computation | loop fusion | flops 8192 | bytes 69632 | tf_op jit(solution)/shard_map/add | solution.py:206
  29.7 1.8 %all-to-all-done.surface = f32[8,8,1152]{2,1,0:T(8,128)S(1)} async-done(((f32[8,8,1152]{2,1,0:T(8,128)}), f32[8,8,1152]{2,1,0:T(8,128)S(1)}, u32[]{:S(2)}, u32[]{:S(2)}) %all-to-all-start) | async-done | bytes 294944 | tf_op jit(solution)/shard_map/all_to_all | solution.py:205
  31.5 7.5 %all-to-all-start.1 = ((f32[8,8,128]{2,1,0:T(8,128)}), f32[8,8,128]{2,1,0:T(8,128)S(1)}, u32[]{:S(2)}, u32[]{:S(2)}) async-start(f32[8,8,128]{2,1,0:T(8,128)} %broadcast_add_fusion), calls=%async_computation.1 | async-start | bytes 65536 | tf_op jit(solution)/shard_map/all_to_all | solution.py:207
  39.0 0.0 copy-done.1
  39.0 2.1 %shard_map.78 = (bf16[8192,128]{1,0:T(8,128)(2,1)S(1)}, bf16[16,8192]{1,0:T(8,128)(2,1)S(1)}, f32[8,128]{1,0:T(8,128)S(1)}) custom-call(f32[3,128]{1,0:T(4,128)S(1)} %copy-done.1, f32[8,8,1152]{2,1,0:T(8,128)S(1)} %all-to-all-done.surface), custom_call_target="tpu_custom_call" | custom-call | flops 5000000000 | bytes 3145728 | tf_op jit(solution)/shard_map/pallas_call | solution.py:209
  41.1 5.9 %all-to-all-done.1.nodes = f32[8,8,128]{2,1,0:T(8,128)S(1)} async-done(((f32[8,8,128]{2,1,0:T(8,128)}), f32[8,8,128]{2,1,0:T(8,128)S(1)}, u32[]{:S(2)}, u32[]{:S(2)}) %all-to-all-start.1) | async-done | bytes 32800 | tf_op jit(solution)/shard_map/all_to_all | solution.py:207
  47.0 0.0 copy-start
  47.0 10.4 %shard_map.79 = (f32[8,8,256]{2,1,0:T(8,128)S(1)}, f32[8,256]{1,0:T(8,128)S(1)}) custom-call(s32[1]{0:T(128)} %bitcast.place, f32[8,8,128]{2,1,0:T(8,128)S(1)} %all-to-all-done.1.nodes, bf16[8192,128]{1,0:T(8,128)(2,1)S(1)} %get-tuple-element.19.right, bf16[16,8192]{1,0:T(8,128)(2,1)S(1)} %get-tuple-element.20.terms, f32[8,128]{1,0:T(8,128)S(1)} %get-tuple-element.21.own_sums), custom_call_target="tpu_custom_call" | custom-call | flops 30000001024 | bytes 3145728 | tf_op jit(solution)/shard_map/pallas_call | solution.py:222
  57.4 10.8 %all_to_all.15.received = f32[8,8,256]{2,1,0:T(8,128)S(1)} all-to-all(f32[8,8,256]{2,1,0:T(8,128)S(1)} %get-tuple-element.22), channel_id=1, replica_groups=mesh['vol'=16,'z'=8,'y'=8] {'y'}, dimensions={0} | all-to-all | bytes 131072 | tf_op jit(solution)/shard_map/all_to_all | solution.py:239
  68.2 0.0 copy-done
  68.2 0.8 %shard_map.80 = (f32[3,128]{1,0:T(4,128)}, f32[4,128]{1,0:T(4,128)}) custom-call(f32[8,8,256]{2,1,0:T(8,128)S(1)} %all_to_all.15.received, f32[8,256]{1,0:T(8,128)S(1)} %get-tuple-element.23.near, s32[4,512]{1,0:T(4,128)S(1)} %copy-done), custom_call_target="tpu_custom_call" | custom-call | tf_op jit(solution)/shard_map/pallas_call | solution.py:241
Async XLA Ops:
  0.6 38.4 %copy-start.1 = (f32[3,128]{1,0:T(4,128)S(1)}, f32[3,128]{1,0:T(4,128)}, u32[]{:S(2)}) copy-start(f32[3,128]{1,0:T(4,128)} %points.3) | copy-start | bytes 4612
  2.2 29.3 %all-to-all-start = ((f32[8,8,1152]{2,1,0:T(8,128)}), f32[8,8,1152]{2,1,0:T(8,128)S(1)}, u32[]{:S(2)}, u32[]{:S(2)}) async-start(f32[8,8,1152]{2,1,0:T(8,128)} %get-tuple-element.14), calls=%async_computation | async-start | bytes 589824 | tf_op jit(solution)/shard_map/all_to_all | solution.py:205
  18.9 9.4 %collective-permute-start = (f32[8,128]{1,0:T(8,128)}, f32[8,128]{1,0:T(8,128)S(1)}, u32[]{:S(2)}, u32[]{:S(2)}) collective-permute-start(f32[8,128]{1,0:T(8,128)} %get-tuple-element.16), channel_id=1, source_target_pairs={{7,8},{8,1},{15,16},{16,9},{23,24},{24,17},{31,32},{32,25},{39,40}... | collective-permute-start | bytes 12296 | tf_op jit(solution)/shard_map/ppermute | solution.py:204
  31.5 15.5 %all-to-all-start.1 = ((f32[8,8,128]{2,1,0:T(8,128)}), f32[8,8,128]{2,1,0:T(8,128)S(1)}, u32[]{:S(2)}, u32[]{:S(2)}) async-start(f32[8,8,128]{2,1,0:T(8,128)} %broadcast_add_fusion), calls=%async_computation.1 | async-start | bytes 65536 | tf_op jit(solution)/shard_map/all_to_all | solution.py:207
  47.0 21.1 %copy-start = (s32[4,512]{1,0:T(4,128)S(1)}, s32[4,512]{1,0:T(4,128)}, u32[]{:S(2)}) copy-start(s32[4,512]{1,0:T(4,128)} %cells.1) | copy-start | bytes 24580

commit v7 on v6

--- a/solution.py
+++ b/solution.py
@@ -129,7 +129,8 @@
     whole = total[:SIDE] + total[SIDE:]
 
     def keep(block, value):
-        message[block, :, :LANES] = value
+        message[block, 0] = value[:4]
+        message[block, 1] = value[4:]
         index = nodes[block][3:4].astype(jnp.int32)
         sums[block + 1] = pick_lanes(value, index)
         spots[block + 1] = pick_lanes(nodes[block], index)
@@ -143,15 +144,25 @@
     spots[0] = outer
     spots[SIDE + 1] = pltpu.roll(outer, LANES - 32, axis=1)
     for block in range(SIDE):
-        message[block, :, LANES:] = jnp.where(lane < 32, sums[block], pltpu.roll(sums[block + 2], 32, axis=1))
+        lent = jnp.where(lane < 32, sums[block], pltpu.roll(sums[block + 2], 32, axis=1))
+        right_half = pltpu.roll(pltpu.roll(lent, 4, axis=0), 64, axis=1)
+        message[block, 2] = jnp.where(lane < 64, lent, right_half)[:4]
     near[:, :LANES] = nodes[here]
     near[:, LANES:] = jnp.where(lane < 32, spots[here], pltpu.roll(spots[here + 2], 32, axis=1))
 
 
 def swept_kernel(received, near, cells, motion_out, swept_out):
-    total = received[0]
+    whole = received[0]
     for i in range(1, SIDE):
-        total = total + received[i]
+        whole = whole + received[i]
+    packed = whole[2]
+    total = jnp.concatenate(
+        [
+            jnp.concatenate([whole[0], whole[1]], axis=0),
+            jnp.concatenate([packed, pltpu.roll(packed, 64, axis=1)], axis=0),
+        ],
+        axis=1,
+    )
     top = [total[i : i + 1] for i in range(3)]
     turn = [total[i : i + 1] for i in range(3, 6)]
     spot = [near[i : i + 1, :] for i in range(5, 8)]
@@ -222,7 +233,7 @@
     partial, near = pl.pallas_call(
         sums_kernel,
         out_shape=(
-            jax.ShapeDtypeStruct((SIDE, 8, 2 * LANES), F32),
+            jax.ShapeDtypeStruct((SIDE, 3, 4, LANES), F32),
             jax.ShapeDtypeStruct((8, 2 * LANES), F32),
         ),
         in_specs=[pl.BlockSpec(memory_space=pltpu.SMEM), vmem, vmem, vmem, vmem],

time: 69.4 us -> 69.3 us (level)
  no operation moved by 1% of the time
where the time goes in v7:
time: 69.3 us; the launch traced here: 68.9 us
  starting transfers between devices  30.2 us (44%)
  Pallas kernels  14.9 us (22%)
  waiting for transfers between devices  11.2 us (16%)
  blocking collectives  10.6 us (15%)
  other arithmetic  1.37 us (2%)
    all_to_all x1, starting transfers between devices, shards(): surfaces = lax.all_to_all(message, 'z', 0, 0)  16.7 us
    all_to_all x1, blocking collectives, shards(): received = lax.all_to_all(partial, 'y', 0, 0)  10.6 us
    pallas_call x1, Pallas kernels, shards(): pl.pallas_call(sums_kernel, out_shape=(jax.ShapeDtypeStruct((SIDE, 3, 4,...  10.4 us
    all_to_all x1, starting transfers between devices, shards(): around = lax.all_to_all(ready, 'y', 0, 0)  7.48 us
    ppermute x1, starting transfers between devices, shards(): outer = lax.ppermute(lent, ('vol', 'z', 'y'), ends)  6.01 us
    all_to_all x1, waiting for transfers between devices, shards(): around = lax.all_to_all(ready, 'y', 0, 0)  5.9 us
    ppermute x1, waiting for transfers between devices, shards(): outer = lax.ppermute(lent, ('vol', 'z', 'y'), ends)  3.43 us
    pallas_call x1, Pallas kernels, shards(): pl.pallas_call(own_kernel, out_shape=(jax.ShapeDtypeStruct((total_surface...  2.12 us
  transfers between devices with their start and end apart: 3, of which 3 were waited for; matrix products, arithmetic and copies ran while one was open for 2% of the time, Pallas kernels for 3%

profile of v7, /device:TPU:14, one launch (start us, length us, event | category | flops | bytes accessed | tf_op | source)
XLA Modules:
  0.0 68.9 jit_solution(5322230328262283300)
XLA Ops:
  0.6 0.0 copy-start.1
  0.6 1.5 %shard_map.77 = (f32[8,8,1152]{2,1,0:T(8,128)}, f32[8,8,128]{2,1,0:T(8,128)}, f32[8,128]{1,0:T(8,128)}) custom-call(f32[3,128]{1,0:T(4,128)} %points.3, f32[3,1024]{1,0:T(4,128)} %surface.1, f32[3,1024]{1,0:T(4,128)} %displacement.1, f32[3,1024]{1,0:T(4,128)} %rotation.1, s32[1,32]{1,0:T(1,128)} %bitcast.4), custom_call_target="tpu_custom_call" | custom-call | flops 3000000000 | bytes 8388608 | tf_op jit(solution)/shard_map/pallas_call | solution.py:200
  2.2 16.7 %all-to-all-start = ((f32[8,8,1152]{2,1,0:T(8,128)}), f32[8,8,1152]{2,1,0:T(8,128)S(1)}, u32[]{:S(2)}, u32[]{:S(2)}) async-start(f32[8,8,1152]{2,1,0:T(8,128)} %get-tuple-element.14), calls=%async_computation | async-start | bytes 589824 | tf_op jit(solution)/shard_map/all_to_all | solution.py:216
  18.9 6.0 %collective-permute-start = (f32[8,128]{1,0:T(8,128)}, f32[8,128]{1,0:T(8,128)S(1)}, u32[]{:S(2)}, u32[]{:S(2)}) collective-permute-start(f32[8,128]{1,0:T(8,128)} %get-tuple-element.16), channel_id=1, source_target_pairs={{7,8},{8,1},{15,16},{16,9},{23,24},{24,17},{31,32},{32,25},{39,40}... | collective-permute-start | bytes 12296 | tf_op jit(solution)/shard_map/ppermute | solution.py:215
  24.9 3.4 %collective-permute-done = f32[8,128]{1,0:T(8,128)S(1)} collective-permute-done((f32[8,128]{1,0:T(8,128)}, f32[8,128]{1,0:T(8,128)S(1)}, u32[]{:S(2)}, u32[]{:S(2)}) %collective-permute-start) | collective-permute-done | bytes 4128 | tf_op jit(solution)/shard_map/ppermute | solution.py:215
  28.3 1.4 %broadcast_add_fusion = f32[8,8,128]{2,1,0:T(8,128)} fusion(f32[8,8,128]{2,1,0:T(8,128)} %get-tuple-element.15, f32[8,128]{1,0:T(8,128)S(1)} %collective-permute-done), kind=kLoop, calls=%fused_computation | loop fusion | flops 8192 | bytes 69632 | tf_op jit(solution)/shard_map/add | solution.py:217
  29.7 1.8 %all-to-all-done.surface = f32[8,8,1152]{2,1,0:T(8,128)S(1)} async-done(((f32[8,8,1152]{2,1,0:T(8,128)}), f32[8,8,1152]{2,1,0:T(8,128)S(1)}, u32[]{:S(2)}, u32[]{:S(2)}) %all-to-all-start) | async-done | bytes 294944 | tf_op jit(solution)/shard_map/all_to_all | solution.py:216
  31.5 7.5 %all-to-all-start.1 = ((f32[8,8,128]{2,1,0:T(8,128)}), f32[8,8,128]{2,1,0:T(8,128)S(1)}, u32[]{:S(2)}, u32[]{:S(2)}) async-start(f32[8,8,128]{2,1,0:T(8,128)} %broadcast_add_fusion), calls=%async_computation.1 | async-start | bytes 65536 | tf_op jit(solution)/shard_map/all_to_all | solution.py:218
  39.0 0.0 copy-done.1
  39.0 2.1 %shard_map.78 = (bf16[8192,128]{1,0:T(8,128)(2,1)S(1)}, bf16[16,8192]{1,0:T(8,128)(2,1)S(1)}, f32[8,128]{1,0:T(8,128)S(1)}) custom-call(f32[3,128]{1,0:T(4,128)S(1)} %copy-done.1, f32[8,8,1152]{2,1,0:T(8,128)S(1)} %all-to-all-done.surface), custom_call_target="tpu_custom_call" | custom-call | flops 5000000000 | bytes 3145728 | tf_op jit(solution)/shard_map/pallas_call | solution.py:220
  41.1 5.9 %all-to-all-done.1.nodes = f32[8,8,128]{2,1,0:T(8,128)S(1)} async-done(((f32[8,8,128]{2,1,0:T(8,128)}), f32[8,8,128]{2,1,0:T(8,128)S(1)}, u32[]{:S(2)}, u32[]{:S(2)}) %all-to-all-start.1) | async-done | bytes 32800 | tf_op jit(solution)/shard_map/all_to_all | solution.py:218
  47.0 0.0 copy-start
  47.0 10.4 %shard_map.79 = (f32[8,3,4,128]{3,2,1,0:T(4,128)S(1)}, f32[8,256]{1,0:T(8,128)S(1)}) custom-call(s32[1]{0:T(128)} %bitcast.place, f32[8,8,128]{2,1,0:T(8,128)S(1)} %all-to-all-done.1.nodes, bf16[8192,128]{1,0:T(8,128)(2,1)S(1)} %get-tuple-element.19.right, bf16[16,8192]{1,0:T(8,128)(2,1)S(1)} %get-tuple-element.20.terms, f32[8,128]{1,0:T(8,128)S(1)} %get-tuple-element.21.own_sums), custom_call_target="tpu_custom_call" | custom-call | flops 30000001024 | bytes 3145728 | tf_op jit(solution)/shard_map/pallas_call | solution.py:233
  57.5 10.6 %all_to_all.15.received = f32[8,3,4,128]{3,2,1,0:T(4,128)S(1)} all-to-all(f32[8,3,4,128]{3,2,1,0:T(4,128)S(1)} %get-tuple-element.22), channel_id=1, replica_groups=mesh['vol'=16,'z'=8,'y'=8] {'y'}, dimensions={0} | all-to-all | bytes 98304 | tf_op jit(solution)/shard_map/all_to_all | solution.py:250
  68.0 0.0 copy-done
  68.0 0.8 %shard_map.80 = (f32[3,128]{1,0:T(4,128)}, f32[4,128]{1,0:T(4,128)}) custom-call(f32[8,3,4,128]{3,2,1,0:T(4,128)S(1)} %all_to_all.15.received, f32[8,256]{1,0:T(8,128)S(1)} %get-tuple-element.23.near, s32[4,512]{1,0:T(4,128)S(1)} %copy-done), custom_call_target="tpu_custom_call" | custom-call | tf_op jit(solution)/shard_map/pallas_call | solution.py:252
Async XLA Ops:
  0.6 38.4 %copy-start.1 = (f32[3,128]{1,0:T(4,128)S(1)}, f32[3,128]{1,0:T(4,128)}, u32[]{:S(2)}) copy-start(f32[3,128]{1,0:T(4,128)} %points.3) | copy-start | bytes 4612
  2.2 29.3 %all-to-all-start = ((f32[8,8,1152]{2,1,0:T(8,128)}), f32[8,8,1152]{2,1,0:T(8,128)S(1)}, u32[]{:S(2)}, u32[]{:S(2)}) async-start(f32[8,8,1152]{2,1,0:T(8,128)} %get-tuple-element.14), calls=%async_computation | async-start | bytes 589824 | tf_op jit(solution)/shard_map/all_to_all | solution.py:216
  18.9 9.4 %collective-permute-start = (f32[8,128]{1,0:T(8,128)}, f32[8,128]{1,0:T(8,128)S(1)}, u32[]{:S(2)}, u32[]{:S(2)}) collective-permute-start(f32[8,128]{1,0:T(8,128)} %get-tuple-element.16), channel_id=1, source_target_pairs={{7,8},{8,1},{15,16},{16,9},{23,24},{24,17},{31,32},{32,25},{39,40}... | collective-permute-start | bytes 12296 | tf_op jit(solution)/shard_map/ppermute | solution.py:215
  31.5 15.5 %all-to-all-start.1 = ((f32[8,8,128]{2,1,0:T(8,128)}), f32[8,8,128]{2,1,0:T(8,128)S(1)}, u32[]{:S(2)}, u32[]{:S(2)}) async-start(f32[8,8,128]{2,1,0:T(8,128)} %broadcast_add_fusion), calls=%async_computation.1 | async-start | bytes 65536 | tf_op jit(solution)/shard_map/all_to_all | solution.py:218
  47.0 21.0 %copy-start = (s32[4,512]{1,0:T(4,128)S(1)}, s32[4,512]{1,0:T(4,128)}, u32[]{:S(2)}) copy-start(s32[4,512]{1,0:T(4,128)} %cells.1) | copy-start | bytes 24580
